TPU v7x, 128 devices: a whole 4x4x4 slice. The times are simulated.
128 devices in a mesh: dp: 16 (over y, x), row: 2 (over core), col: 4 (over z).
Axes of the slice: x: 4, y: 4, z: 4, core: 2. Of those that a mesh axis runs over, the one named last changes fastest.
Arguments:
- hidden: bfloat16 [16384, 14336], P('dp', 'row'), may hold values from -6 to 6
- upstream: bfloat16 [16384, 4096], P('dp', 'col'), may hold values from -0.046875 to 0.046875
- first_codes: int32 [14336, 4096], P(('row', 'dp'), 'col'), may hold values from 0 to 15
- first_scale: float32 [14336, 32], P(('row', 'dp'), 'col'), may hold values from 0.1 to 1
- second_codes: int32 [14336, 4096], P(('row', 'dp'), 'col'), may hold values from 0 to 15
- second_rows: float32 [14336], P(('row', 'dp')), may hold values from 0.004 to 0.04
- second_columns: float32 [4096], P('col'), may hold values from 0.004 to 0.04
Outputs:
- update_step: float32 [14336, 4096], P(('row', 'dp'), 'col')
- first_normed: bfloat16 [14336, 4096], P(('row', 'dp'), 'col')
- first_peak: float32 [14336, 32], P(('row', 'dp'), 'col')
- second_normed: bfloat16 [14336, 4096], P(('row', 'dp'), 'col')
- row_peak: float32 [14336], P(('row', 'dp'))
- column_peak: float32 [4096], P('col')
All inputs are finite; a program needn't handle non-finite values. Where the computation divides by a largest or mean magnitude, that divisor is 1e-20 or more.
Results may differ from a plain program's by a relative error of at most 0.015.
Values may be sent and summed in bfloat16 or wider, within the bound.
No kernel may reach another device: no remote copies, remote signals or barrier semaphores. Data moves between devices by JAX's collectives and lax.ppermute only.
A program may use at most 128 MiB of HBM per device.

v0:
```python
import jax
import jax.numpy as jnp
from jax import lax
from jax.sharding import PartitionSpec as P

STEP = 10


def first_table(codes):
    level = codes.astype(jnp.float32)
    upper = level >= 8.0
    expo = jnp.where(upper, level - 8.0, 7.0 - level)
    magnitude = jnp.where(expo > 0.0, jnp.exp2(expo - 7.0), 0.0 * expo)
    return jnp.where(upper, magnitude, -magnitude)


def contract_tokens(left, right):
    return lax.dot_general(
        left, right, (((0,), (0,)), ((), ())), preferred_element_type=jnp.float32
    )


def per_device(
    hidden, upstream, first_codes, first_scale, second_codes, second_rows, second_columns
):
    rows_own = first_codes.shape[0]
    columns = first_codes.shape[1]
    block_count = first_scale.shape[1]
    partial_value = contract_tokens(hidden, upstream)
    summed = lax.psum(partial_value.astype(jnp.bfloat16), "dp").astype(jnp.float32)
    gradient = lax.dynamic_slice_in_dim(summed, lax.axis_index("dp") * rows_own, rows_own, 0)
    shaped = gradient.reshape(rows_own, block_count, -1)
    first_old = first_scale[:, :, None] * first_table(first_codes).reshape(
        rows_own, block_count, -1
    )
    level_two = (second_codes.astype(jnp.float32) + 1.0) / 16.0
    second_old = (jnp.minimum(second_rows[:, None], second_columns[None, :]) * level_two).reshape(
        rows_own, block_count, -1
    )
    first_new = 0.9 * first_old + 0.1 * shaped
    second_new = 0.999 * second_old + 0.001 * shaped * shaped
    corr_one = 1.0 - 0.9**STEP
    corr_two = 1.0 - 0.999**STEP
    update_step = first_new / corr_one / (jnp.sqrt(second_new / corr_two) + 1e-08)
    first_peak = jnp.max(jnp.abs(first_new), axis=2)
    first_normed = (first_new / (first_peak[:, :, None] + 1e-06)).astype(jnp.bfloat16)
    second_flat = second_new.reshape(rows_own, columns)
    row_part = jnp.max(second_flat, axis=1)
    column_part = jnp.max(second_flat, axis=0)
    row_peak = lax.pmax(row_part, "col")
    column_peak = lax.pmax(column_part, ("dp", "row"))
    second_normed = (
        second_flat / (jnp.minimum(row_peak[:, None], column_peak[None, :]) + 1e-06)
    ).astype(jnp.bfloat16)
    return (
        update_step.reshape(rows_own, columns),
        first_normed.reshape(rows_own, columns),
        first_peak,
        second_normed,
        row_peak,
        column_peak,
    )


def solution(mesh):
    placed = (
        P("dp", "row"),
        P("dp", "col"),
        P(("row", "dp"), "col"),
        P(("row", "dp"), "col"),
        P(("row", "dp"), "col"),
        P(("row", "dp")),
        P("col"),
    )
    return jax.shard_map(
        per_device,
        mesh=mesh,
        in_specs=placed,
        out_specs=(
            P(("row", "dp"), "col"),
            P(("row", "dp"), "col"),
            P(("row", "dp"), "col"),
            P(("row", "dp"), "col"),
            P(("row", "dp")),
            P("col"),
        ),
        check_vma=False,
    )
```

profile of v0, /device:TPU:0, one launch (start us, length us, event | category | flops | bytes accessed | tf_op | source)
XLA Modules:
  0.0 330.0 jit_solution(2159188544943011163)
XLA Ops:
  7.2 0.0 copy-start
  7.2 0.0 all-reduce.2.cloned.1.call-start
  7.2 1.5 copy-done
  8.8 23.9 %convolution_convert_fusion = bf16[7168,1024]{1,0:T(8,128)(2,1)} fusion(bf16[1024,7168]{1,0:T(8,128)(2,1)} %param.7, bf16[1024,1024]{1,0:T(8,128)(2,1)S(1)} %copy-done), kind=kOutput, calls=%fused_computation | convolution fusion | flops 15039725568 | bytes 31457280 | tf_op jit(solution)/shard_map/dot_general | solution.py:18
  32.7 0.0 copy-start.2
  32.7 0.0 all-reduce.2.cloned.1.call-update
  32.7 1.5 copy-done.2
  34.2 0.8 fusion.7
  35.0 0.0 copy-start.6
  35.0 0.0 copy-start.8
  35.1 0.0 copy-start.9
  35.1 0.4 copy.18
  35.5 0.3 copy-done.6
  35.8 0.1 copy.15
  35.9 198.2 %all-reduce.2.cloned.1.call-done = bf16[7168,1024]{1,0:T(8,128)(2,1)} async-done(((bf16[7168,1024]{1,0:T(8,128)(2,1)}), bf16[7168,1024]{1,0:T(8,128)(2,1)}) %all-reduce.2.cloned.1.call-update) | async-done | bytes 14680080 | tf_op jit(solution)/shard_map/psum | solution.py:30
  234.1 0.0 copy-done.8
  234.1 0.0 copy-done.9
  234.1 3.8 %fusion.8 = (f32[448]{0:T(512)S(1)}, f32[1024]{0:T(1024)S(1)}, f32[448,1024]{1,0:T(8,128)}, f32[56,8,8,128]{3,1,2,0:T(8,128)S(1)}) fusion(bf16[7168,1024]{1,0:T(8,128)(2,1)} %all-reduce.2.cloned.1.call-done, s32[]{:T(128)S(6)} %select_n.16, s32[448,1024]{1,0:T(8,128)} %param.11, f32[1024]{0:T(1024)S(1)} %copy-done.8, f32[448]{0:T(512)S(1)} %copy-done.9), kind=kLoop, calls=%fused_computation.22 | loop fusion | flops 5962304 | bytes 6434308 | tf_op jit(solution)/shard_map/reduce_max | solution.py:48
  237.9 0.4 copy.19
  238.3 0.6 bitcast_add_fusion
  238.9 0.5 abs_reduce_fusion
  239.5 0.7 copy.16
  240.2 64.9 %pmax.15 = f32[1024]{0:T(1024)S(1)} all-reduce(f32[1024]{0:T(1024)S(1)} %get-tuple-element.13), channel_id=1, replica_groups=mesh['dp'=16,'row'=2,'col'=4] {'dp','row'}, use_global_device_ids=true, to_apply=%region_5.6 | all-reduce | flops 1024 | bytes 8192 | tf_op jit(solution)/shard_map/pmax | solution.py:51
  305.0 0.0 copy-start.5
  305.1 10.7 %pmax.14 = f32[448]{0:T(512)S(1)} all-reduce(f32[448]{0:T(512)S(1)} %get-tuple-element.12), channel_id=1, replica_groups=mesh['dp'=16,'row'=2,'col'=4] {'col'}, use_global_device_ids=true, to_apply=%region_3.4 | all-reduce | flops 448 | bytes 3584 | tf_op jit(solution)/shard_map/pmax | solution.py:50
  315.7 0.0 copy-start.7
  315.7 0.0 copy-start.3
  315.7 0.0 copy-start.4
  315.8 0.5 div.43
  316.3 0.5 mul.67
  316.8 0.0 copy-done.5
  316.8 0.0 copy-done.7
  316.8 0.4 copy-done.3
  317.2 0.6 copy-done.4
  317.8 0.0 copy-start.1
  317.8 5.3 %fusion.3 = (bf16[448,1024]{1,0:T(8,128)(2,1)}, f32[448,1024]{1,0:T(8,128)}, bf16[448,1024]{1,0:T(8,128)(2,1)}) fusion(f32[56,8,8,128]{3,2,1,0:T(8,128)S(1)} %bitcast.30, bf16[7168,1024]{1,0:T(8,128)(2,1)} %all-reduce.2.cloned.1.call-done, s32[]{:T(128)S(6)} %select_n.16, s32[448,1024]{1,0:T(8,128)S(1)} %copy-done.3, f32[56,8,8,128]{3,2,1,0:T(8,128)S(1)} %bitcast.31, ...), kind=kLoop, calls=%fused_computation.8 | loop fusion | flops 12386304 | bytes 11933444 | tf_op jit(solution)/shard_map/convert_element_type | solution.py:46
  323.1 0.0 copy-done.1
  (1 shorter events, 0.0 us)
Async XLA Ops:
  7.2 1.6 copy-start
  7.2 226.9 %all-reduce.2.cloned.1.call-start = ((), (), s32[]{:S(2)}) async-start(), calls=%async_computation | async-start | bytes 29360128 | tf_op jit(solution)/shard_map/psum | solution.py:30
  32.7 1.5 copy-start.2
  35.0 0.7 copy-start.6
  35.0 199.0 %copy-start.8 = (f32[1024]{0:T(1024)S(1)}, f32[1024]{0:T(1024)}, u32[]{:S(2)}) copy-start(f32[1024]{0:T(1024)} %param.13) | copy-start | bytes 12292
  35.1 199.0 %copy-start.9 = (f32[448]{0:T(512)S(1)}, f32[448]{0:T(512)}, u32[]{:S(2)}) copy-start(f32[448]{0:T(512)} %param.12) | copy-start | bytes 5380
  305.0 11.8 %copy-start.5 = (f32[1024]{0:T(1024)}, f32[1024]{0:T(1024)S(1)}, u32[]{:S(2)}) copy-start(f32[1024]{0:T(1024)S(1)} %pmax.15) | copy-start | bytes 12292
  315.7 1.1 copy-start.7
  315.7 1.5 copy-start.3
  315.7 2.1 copy-start.4
  317.8 5.3 %copy-start.1 = (bf16[1024,1024]{1,0:T(8,128)(2,1)S(1)}, bf16[1024,1024]{1,0:T(8,128)(2,1)}, u32[]{:S(2)}) copy-start(bf16[1024,1024]{1,0:T(8,128)(2,1)} %param.8) | copy-start | bytes 6291460
Sparse Core Ops, SparseCore 0:
  32.8 201.1 all-reduce.1
where the time goes:
time: 330 us
  waiting for transfers between devices  198 us (60%)
  blocking collectives  75.6 us (23%)
  matrix products  23.9 us (7%)
  between operations  14.1 us (4%)
  other arithmetic  11.1 us (3%)
  local copies, waits for them, and re-layouts  6.97 us (2%)
    psum x1, waiting for transfers between devices, per_device(): lax.psum(partial_value.astype(jnp.bfloat16), 'dp').astype(jnp.float32)  198 us
    pmax x1, blocking collectives, per_device(): column_peak = lax.pmax(column_part, ('dp', 'row'))  64.9 us
    dot_general x1, matrix products, contract_tokens(): lax.dot_general(left, right, (((0,), (0,)), ((), ())), preferred_element_...  23.9 us
    pmax x1, blocking collectives, per_device(): row_peak = lax.pmax(row_part, 'col')  10.7 us
  transfers between devices with their start and end apart: 1, of which 1 were waited for; matrix products, arithmetic and copies ran while one was open for 0% of the time, Pallas kernels for 0%

commit v1 on v0

v1 whole, which is shorter than its diff:
```python
import functools

import jax
import jax.numpy as jnp
from jax import lax
from jax.experimental import pallas as pl
from jax.experimental.pallas import tpu as pltpu
from jax.sharding import PartitionSpec as P


STEP = 10
F32 = jnp.float32
BF16 = jnp.bfloat16
OWN = 448
HALF = 512
SPAN = 512
LANES = 128
CORR_ONE = 1.0 - 0.9**STEP
CORR_TWO = 1.0 - 0.999**STEP
ANY = pl.BlockSpec(memory_space=pl.ANY)


GRANT = pltpu.CompilerParams(vmem_limit_bytes=58 << 20)


def dot(left, right):
    return lax.dot_general(left, right, (((0,), (0,)), ((), ())), preferred_element_type=F32)


def product_kernel(base, added, where, hidden, upstream, *refs):
    received = refs[:2] if added else ()
    outs = refs[len(received) : len(received) + 2]
    held, features, got, made, total, sems = refs[len(received) + 2 :]
    loads = [
        pltpu.make_async_copy(
            hidden.at[:, pl.ds(pl.multiple_of(where[base + i] * LANES, LANES), SPAN)],
            held.at[i],
            sems.at[i],
        )
        for i in range(4)
    ]
    feature_copy = pltpu.make_async_copy(upstream, features, sems.at[4])
    got_copies = [
        pltpu.make_async_copy(received[d], got.at[d], sems.at[5 + d]) for d in range(len(received))
    ]
    feature_copy.start()
    for copy in loads:
        copy.start()
    for copy in got_copies:
        copy.start()
    feature_copy.wait()
    stores = []
    for i in range(4):
        loads[i].wait()
        total[i % 2] = dot(held[i], features[...])
        start = pl.multiple_of(where[16 + base + i], 64)
        if i == 0:
            for copy in got_copies:
                copy.wait()
        for d in range(2):
            value = total[i % 2, pl.ds(start, OWN), d * HALF : (d + 1) * HALF]
            if added:
                value = value + got[d, i].astype(F32)
            made[d, i] = value.astype(BF16)
            copy = pltpu.make_async_copy(made.at[d, i], outs[d].at[i], sems.at[7 + 2 * i + d])
            copy.start()
            stores.append(copy)
    for copy in stores:
        copy.wait()


def product(hidden, upstream, where, base, received=()):
    tokens, width = upstream.shape
    piece = jax.ShapeDtypeStruct((4, OWN, HALF), BF16)
    return pl.pallas_call(
        functools.partial(product_kernel, base, bool(received)),
        out_shape=(piece, piece),
        grid_spec=pltpu.PrefetchScalarGridSpec(
            num_scalar_prefetch=1,
            grid=(1,),
            in_specs=[ANY] * (2 + len(received)),
            out_specs=(ANY, ANY),
            scratch_shapes=[
                pltpu.VMEM((4, tokens, SPAN), BF16),
                pltpu.VMEM((tokens, width), BF16),
                pltpu.VMEM((2, 4, OWN, HALF) if received else (2, 1, 16, 128), BF16),
                pltpu.VMEM((2, 4, OWN, HALF), BF16),
                pltpu.VMEM((2, SPAN, width), F32),
                pltpu.SemaphoreType.DMA((15,)),
            ],
        ),
        cost_estimate=pl.CostEstimate(
            flops=8 * OWN * tokens * width, bytes_accessed=10 << 20, transcendentals=0
        ),
        compiler_params=GRANT,
    )(where, hidden, upstream, *received)


def ring(first_core, k):
    pairs = []
    for y in range(4):
        for x in range(4):
            for core in range(2):
                along_x = core == first_core
                to = 4 * y + (x + k) % 4 if along_x else 4 * ((y + k) % 4) + x
                pairs.append((2 * (4 * y + x) + core, 2 * to + core))
    return pairs


def near(k):
    return ring(0, k)


def other(k):
    return ring(1, k)


def send(value, pairs):
    return lax.ppermute(value, ("dp", "row"), pairs)


def sum_kernel(kept, got, far, up, down, held, made, sems):
    outs = (far, up, down)
    loads = [
        [
            pltpu.make_async_copy(a.at[k], held.at[k, n], sems.at[2 * k + n])
            for n, a in enumerate((kept, got))
        ]
        for k in range(3)
    ]
    for group in loads:
        for copy in group:
            copy.start()
    stores = []
    for k in range(3):
        for copy in loads[k]:
            copy.wait()
        made[k] = (held[k, 0].astype(F32) + held[k, 1].astype(F32)).astype(BF16)
        copy = pltpu.make_async_copy(made.at[k], outs[k], sems.at[6 + k])
        copy.start()
        stores.append(copy)
    for copy in stores:
        copy.wait()


def last(kept, got):
    message = jax.ShapeDtypeStruct((OWN, HALF), BF16)
    far, up, down = pl.pallas_call(
        sum_kernel,
        out_shape=(message,) * 3,
        in_specs=[ANY] * 2,
        out_specs=(ANY,) * 3,
        scratch_shapes=[
            pltpu.VMEM((3, 2, OWN, HALF), BF16),
            pltpu.VMEM((3, OWN, HALF), BF16),
            pltpu.SemaphoreType.DMA((9,)),
        ],
        cost_estimate=pl.CostEstimate(
            flops=3 * OWN * HALF, bytes_accessed=4 << 20, transcendentals=0
        ),
        compiler_params=GRANT,
    )(kept, got)
    return (send(far, other(2)), send(up, other(1)), send(down, other(-1)))


def add(left, right):
    return (left.astype(F32) + right.astype(F32)).astype(BF16)


def reduced(hidden, upstream, owner):
    owners = jnp.stack([owner(p, q) for p in (2, 1, 3, 0) for q in (2, 1, 3, 0)])
    where = jnp.concatenate([(7 * owners) >> 1, 64 * (owners & 1)]).astype(jnp.int32)
    far_low, far_high = product(hidden, upstream, where, 0)
    from_low = send(far_low, near(1))
    from_high = send(far_high, near(-1))
    up_low, up_high = product(hidden, upstream, where, 4)
    direct_high = send(up_high, near(1))
    down_low, down_high = product(hidden, upstream, where, 8)
    direct_low = send(down_low, near(-1))
    added_low = send(add(up_low[:3], from_low[:3]), near(1))
    added_high = send(add(down_high[:3], from_high[:3]), near(-1))
    added_low_own = send(add(up_low[3], from_low[3]), near(1))
    added_high_own = send(add(down_high[3], from_high[3]), near(-1))
    own_low, own_high = product(hidden, upstream, where, 12, (direct_low, direct_high))
    return (
        (own_low, added_low_own, *last(own_low, added_low)),
        (own_high, added_high_own, *last(own_high, added_high)),
    )


TALL = 112
CHUNKS = OWN // TALL


def second_kernel(half, own, added, far, up, down, codes, rows, columns, *refs):
    before, refs = (refs[:2], refs[2:]) if half else ((), refs)
    gradient, second, row_out, column_out = refs[:4]
    parts, code, row, column, made, wide, sems = refs[4:]
    here = pl.ds(half * HALF, HALF)
    small = [
        pltpu.make_async_copy(rows, row, sems.at[0]),
        pltpu.make_async_copy(columns.at[:, here], column, sems.at[1]),
    ]
    loads = []
    for i in range(CHUNKS):
        at = pl.ds(i * TALL, TALL)
        sources = [own.at[3, at], added.at[at], far.at[at], up.at[at], down.at[at]]
        group = [
            pltpu.make_async_copy(a, parts.at[n, at], sems.at[2 + 6 * i + n])
            for n, a in enumerate(sources)
        ]
        group.append(
            pltpu.make_async_copy(codes.at[at, here], code.at[at], sems.at[2 + 6 * i + 5])
        )
        loads.append(group)
    for copy in small:
        copy.start()
    for group in loads:
        for copy in group:
            copy.start()
    for copy in small:
        copy.wait()
    peak = None
    stores = []
    for i in range(CHUNKS):
        at = pl.ds(i * TALL, TALL)
        for copy in loads[i]:
            copy.wait()
        total = parts[0, at, :].astype(F32)
        for n in range(1, 5):
            total = total + parts[n, at, :].astype(F32)
        level = (code[at, :].astype(F32) + 1.0) / 16.0
        old = jnp.minimum(row[at, :], column[...]) * level
        new = 0.999 * old + 0.001 * total * total
        made[0, at, :] = total
        made[1, at, :] = new
        for n, out in enumerate((gradient, second)):
            copy = pltpu.make_async_copy(
                made.at[n, at], out.at[at], sems.at[2 + 6 * CHUNKS + 2 * i + n]
            )
            copy.start()
            stores.append(copy)
        top = jnp.max(new, axis=0, keepdims=True)
        peak = top if peak is None else jnp.maximum(peak, top)
        widest = new[:, :LANES]
        for b in range(1, HALF // LANES):
            widest = jnp.maximum(widest, new[:, b * LANES : (b + 1) * LANES])
        wide[at, :] = widest
    row_top = jnp.max(wide[...].T, axis=0, keepdims=True)
    if half:
        row_out[...] = jnp.maximum(row_top, before[0][...])
        column_out[:, :HALF] = before[1][...]
        column_out[:, HALF:] = peak
    else:
        row_out[...] = row_top
        column_out[...] = peak
    for copy in stores:
        copy.wait()


def second_moment(half, parts, codes, rows, columns, before=()):
    vmem = pl.BlockSpec(memory_space=pltpu.MemorySpace.VMEM)
    reach = HALF * (1 + half)
    return pl.pallas_call(
        functools.partial(second_kernel, half),
        out_shape=(
            jax.ShapeDtypeStruct((OWN, HALF), F32),
            jax.ShapeDtypeStruct((OWN, HALF), F32),
            jax.ShapeDtypeStruct((1, OWN), F32),
            jax.ShapeDtypeStruct((1, reach), F32),
        ),
        in_specs=[ANY] * 8 + [vmem] * len(before),
        out_specs=(ANY, ANY, vmem, vmem),
        scratch_shapes=[
            pltpu.VMEM((5, OWN, HALF), BF16),
            pltpu.VMEM((OWN, HALF), jnp.int32),
            pltpu.VMEM((OWN, 1), F32),
            pltpu.VMEM((1, HALF), F32),
            pltpu.VMEM((2, OWN, HALF), F32),
            pltpu.VMEM((OWN, LANES), F32),
            pltpu.SemaphoreType.DMA((2 + 8 * CHUNKS,)),
        ],
        cost_estimate=pl.CostEstimate(
            flops=20 * OWN * HALF, bytes_accessed=5 << 20, transcendentals=0
        ),
        compiler_params=GRANT,
    )(*parts, codes, rows, columns, *before)


def first_kernel(half, gradient, second, codes, scale, *refs):
    update, normed, peaks = refs[-3:]
    blocks = HALF // LANES
    for b in range(blocks):
        here = slice(b * LANES, (b + 1) * LANES)
        block = half * blocks + b
        code = codes[:, here]
        upper = code >= 8
        expo = jnp.where(upper, code - 8, 7 - code)
        magnitude = jnp.where(expo > 0, lax.shift_left(jnp.ones_like(expo), expo), 0)
        table = jnp.where(upper, magnitude, -magnitude).astype(F32) * (1.0 / 128.0)
        new = 0.9 * (scale[:, block : block + 1] * table) + 0.1 * gradient[:, here]
        update[:, here] = new / CORR_ONE / (jnp.sqrt(second[:, here] / CORR_TWO) + 1e-08)
        peak = jnp.max(jnp.abs(new), axis=1, keepdims=True)
        normed[:, here] = (new / (peak + 1e-06)).astype(BF16)
        peaks[:, block : block + 1] = peak
    for b in range(blocks):
        kept = (1 - half) * blocks + b
        if half:
            peaks[:, kept : kept + 1] = refs[0][:, kept : kept + 1]
        else:
            peaks[:, kept : kept + 1] = jnp.zeros((peaks.shape[0], 1), F32)


def first_moment(half, gradient, second, codes, scale, before=()):
    rows, width = codes.shape
    blocks = scale.shape[1]
    half_spec = pl.BlockSpec((TALL, HALF), lambda i: (i, 0))
    there_spec = pl.BlockSpec((TALL, HALF), lambda i: (i, half))
    peak_spec = pl.BlockSpec((TALL, blocks), lambda i: (i, 0))
    return pl.pallas_call(
        functools.partial(first_kernel, half),
        out_shape=(
            jax.ShapeDtypeStruct((rows, width), F32),
            jax.ShapeDtypeStruct((rows, width), BF16),
            jax.ShapeDtypeStruct((rows, blocks), F32),
        ),
        grid=(CHUNKS,),
        in_specs=[half_spec, half_spec, there_spec, peak_spec]
        + ([peak_spec, ANY, ANY] if half else []),
        out_specs=(there_spec, there_spec, peak_spec),
        input_output_aliases={5: 0, 6: 1} if half else {},
        cost_estimate=pl.CostEstimate(
            flops=40 * rows * HALF, bytes_accessed=5 << 20, transcendentals=rows * HALF
        ),
        compiler_params=GRANT,
    )(gradient, second, codes, scale, *before)


def norm_kernel(low, high, row_peak, column_peak, normed):
    rows = low.shape[0]
    row = jnp.broadcast_to(row_peak[...], (LANES, rows)).T
    for n, second in enumerate((low, high)):
        for b in range(HALF // LANES):
            here = slice(b * LANES, (b + 1) * LANES)
            there = slice(n * HALF + b * LANES, n * HALF + (b + 1) * LANES)
            peak = jnp.minimum(row, column_peak[:, there]) + 1e-06
            normed[:, there] = (second[:, here] / peak).astype(BF16)


def norm_second(low, high, row_peak, column_peak):
    return pl.pallas_call(
        norm_kernel,
        out_shape=jax.ShapeDtypeStruct((OWN, 2 * HALF), BF16),
        compiler_params=GRANT,
        name="norm",
    )(low, high, row_peak, column_peak)


def ring_max(value, axis, way):
    parts = []
    for k in (1, 2, 3):
        parts.append(lax.ppermute(value, axis, way(k)))
    for part in parts:
        value = jnp.maximum(value, part)
    return value


def per_device(
    hidden, upstream, first_codes, first_scale, second_codes, second_rows, second_columns
):
    dp, core = lax.axis_index("dp"), lax.axis_index("row")
    x, y = dp & 3, dp >> 2

    def owner(p, q):
        along_x, along_y = jnp.where(core == 0, p, q), jnp.where(core == 0, q, p)
        return 4 * ((y + along_y) & 3) + ((x + along_x) & 3)

    low, high = reduced(hidden, upstream, owner)
    rows, columns = second_rows[:, None], second_columns[None, :]
    gradient_low, second_low, row_low, column_low = second_moment(
        0, low, second_codes, rows, columns
    )
    done = first_moment(0, gradient_low, second_low, first_codes, first_scale)
    gradient_high, second_high, row_peak, column_peak = second_moment(
        1, high, second_codes, rows, columns, (row_low, column_low)
    )
    both = ("dp", "row")
    partner = lax.ppermute(column_peak, "row", [(0, 1), (1, 0)])
    for k in (1, 2):
        beside = lax.ppermute(row_peak, "col", [(z, z ^ k) for z in range(4)])
        row_peak = jnp.maximum(row_peak, beside)
    column_peak = ring_max(jnp.maximum(column_peak, partner), both, near)
    column_peak = ring_max(column_peak, both, other)
    update_step, first_normed, first_peak = first_moment(
        1, gradient_high, second_high, first_codes, first_scale, (done[2], done[0], done[1])
    )
    second_normed = norm_second(second_low, second_high, row_peak, column_peak)
    return (
        update_step,
        first_normed,
        first_peak,
        second_normed,
        row_peak.reshape(-1),
        column_peak.reshape(-1),
    )


def solution(mesh):
    placed = (
        P("dp", "row"),
        P("dp", "col"),
        P(("row", "dp"), "col"),
        P(("row", "dp"), "col"),
        P(("row", "dp"), "col"),
        P(("row", "dp")),
        P("col"),
    )
    return jax.shard_map(
        per_device,
        mesh=mesh,
        in_specs=placed,
        out_specs=(
            P(("row", "dp"), "col"),
            P(("row", "dp"), "col"),
            P(("row", "dp"), "col"),
            P(("row", "dp"), "col"),
            P(("row", "dp")),
            P("col"),
        ),
        check_vma=False,
    )
```

time: 330 us -> 142 us (0.43)
  waiting for transfers between devices: 198 us -> 25.9 us
  blocking collectives: 75.6 us -> 0 us
  Pallas kernels: 0 us -> 62.7 us
  starting transfers between devices: 0.04 us -> 34.7 us
  matrix products: 23.9 us -> 0 us
  between operations: 14.1 us -> 0.96 us
    psum x1 -> x0, waiting for transfers between devices: 198 us -> none  [per_device(): lax.psum(partial_value.astype(jnp.bfloat16), 'dp').astype(jnp.float32)]
    pmax x2 -> x0, blocking collectives: 75.6 us -> none  [the longest x1 64.9 us: per_device(): column_peak = lax.pmax(column_part, ('dp', 'row'))]
    pallas_call x0 -> x11, Pallas kernels: none -> 62.7 us  [the longest x4 37.4 us: product(): pl.pallas_call(functools.partial(product_kernel, base, bool(received)), o...]
    ppermute x0 -> x23, starting transfers between devices: none -> 34.7 us  [the longest x14 21.2 us: send(): return lax.ppermute(value, ('dp', 'row'), pairs)]
    ppermute x0 -> x23, waiting for transfers between devices: none -> 25.9 us  [the longest x14 22.5 us: send(): return lax.ppermute(value, ('dp', 'row'), pairs)]
    dot_general x1 -> x0, matrix products: 23.9 us -> none  [contract_tokens(): lax.dot_general(left, right, (((0,), (0,)), ((), ())), preferred_element_...]
    reduce_max x2 -> x0, other arithmetic: 4.39 us -> none  [the longest x1 3.84 us: per_device(): row_part = jnp.max(second_flat, axis=1)]
    convert_element_type x1 -> x4, other arithmetic: 5.32 us -> 8.11 us  [add(): return (left.astype(F32) + right.astype(F32)).astype(BF16)]
  transfers between devices with their start and end apart: 1 -> 23, of which waited for: 1 -> 9; matrix products, arithmetic and copies ran while one was open for 0% -> 9% of each run, Pallas kernels for 0% -> 33%
where the time goes in v1:
time: 142 us; the launch traced here: 141 us
  Pallas kernels  62.7 us (44%)
  starting transfers between devices  34.7 us (24%)
  waiting for transfers between devices  25.9 us (18%)
  other arithmetic  11.3 us (8%)
  local copies, waits for them, and re-layouts  5.43 us (4%)
    pallas_call x4, Pallas kernels, product(): pl.pallas_call(functools.partial(product_kernel, base, bool(received)), o...  37.4 us
    ppermute x14, waiting for transfers between devices, send(): return lax.ppermute(value, ('dp', 'row'), pairs)  22.5 us
    ppermute x14, starting transfers between devices, send(): return lax.ppermute(value, ('dp', 'row'), pairs)  21.2 us
    pallas_call x2, Pallas kernels, first_moment(): pl.pallas_call(functools.partial(first_kernel, half), out_shape=(jax.Shap...  8.81 us
    pallas_call x2, Pallas kernels, second_moment(): pl.pallas_call(functools.partial(second_kernel, half), out_shape=(jax.Sha...  8.41 us
    convert_element_type x4, other arithmetic, add(): return (left.astype(F32) + right.astype(F32)).astype(BF16)  8.11 us
    ppermute x6, starting transfers between devices, ring_max(): parts.append(lax.ppermute(value, axis, way(k)))  7.57 us
    ppermute x2, starting transfers between devices, per_device(): beside = lax.ppermute(row_peak, 'col', [(z, z ^ k) for z in range(4)])  5.81 us
  transfers between devices with their start and end apart: 23, of which 9 were waited for; matrix products, arithmetic and copies ran while one was open for 9% of the time, Pallas kernels for 33%

profile of v1, /device:TPU:0, one launch (start us, length us, event | category | flops | bytes accessed | tf_op | source)
XLA Modules:
  0.0 140.9 jit_solution(2792547322933425050)
XLA Ops:
  0.7 0.1 stack.67
  0.8 0.6 pad_add_fusion.where
  1.4 9.0 %shard_map.121 = (bf16[4,448,512]{2,1,0:T(8,128)(2,1)}, bf16[4,448,512]{2,1,0:T(8,128)(2,1)}) custom-call(s32[32]{0:T(128)} %pad_add_fusion.where, bf16[1024,7168]{1,0:T(8,128)(2,1)} %hidden.7, bf16[1024,1024]{1,0:T(8,128)(2,1)} %upstream.7), custom_call_target="tpu_custom_call" | custom-call | flops 3758096384 | bytes 10485760 | tf_op jit(solution)/shard_map/pallas_call | solution.py:75
  10.4 1.7 %collective-permute-start.8 = (bf16[4,448,512]{2,1,0:T(8,128)(2,1)}, bf16[4,448,512]{2,1,0:T(8,128)(2,1)}, u32[]{:S(2)}, u32[]{:S(2)}) collective-permute-start(bf16[4,448,512]{2,1,0:T(8,128)(2,1)} %get-tuple-element.44), channel_id=1, source_target_pairs={{0,8},{4,36},{8,16},{12,44},{16,24},{20,52},{24,0},{28,60},{32,40}... | collective-permute-start | bytes 5505032 | tf_op jit(solution)/shard_map/ppermute | solution.py:119
  12.1 1.6 %collective-permute-start.2 = (bf16[4,448,512]{2,1,0:T(8,128)(2,1)}, bf16[4,448,512]{2,1,0:T(8,128)(2,1)S(1)}, u32[]{:S(2)}, u32[]{:S(2)}) collective-permute-start(bf16[4,448,512]{2,1,0:T(8,128)(2,1)} %get-tuple-element.38), channel_id=1, source_target_pairs={{0,24},{4,100},{8,0},{12,108},{16,8},{20,116},{24,16},{28,124},{32... | collective-permute-start | bytes 5505032 | tf_op jit(solution)/shard_map/ppermute | solution.py:119
  13.8 9.0 %shard_map.119 = (bf16[4,448,512]{2,1,0:T(8,128)(2,1)}, bf16[4,448,512]{2,1,0:T(8,128)(2,1)}) custom-call(s32[32]{0:T(128)} %pad_add_fusion.where, bf16[1024,7168]{1,0:T(8,128)(2,1)} %hidden.7, bf16[1024,1024]{1,0:T(8,128)(2,1)} %upstream.7), custom_call_target="tpu_custom_call" | custom-call | flops 3758096384 | bytes 10485760 | tf_op jit(solution)/shard_map/pallas_call | solution.py:75
  22.8 0.6 collective-permute-start.1
  23.4 9.0 %shard_map.118 = (bf16[4,448,512]{2,1,0:T(8,128)(2,1)}, bf16[4,448,512]{2,1,0:T(8,128)(2,1)}) custom-call(s32[32]{0:T(128)} %pad_add_fusion.where, bf16[1024,7168]{1,0:T(8,128)(2,1)} %hidden.7, bf16[1024,1024]{1,0:T(8,128)(2,1)} %upstream.7), custom_call_target="tpu_custom_call" | custom-call | flops 3758096384 | bytes 10485760 | tf_op jit(solution)/shard_map/pallas_call | solution.py:75
  32.4 2.9 %collective-permute-start = (bf16[4,448,512]{2,1,0:T(8,128)(2,1)}, bf16[4,448,512]{2,1,0:T(8,128)(2,1)S(1)}, u32[]{:S(2)}, u32[]{:S(2)}) collective-permute-start(bf16[4,448,512]{2,1,0:T(8,128)(2,1)} %get-tuple-element.34), channel_id=1, source_target_pairs={{0,24},{4,100},{8,0},{12,108},{16,8},{20,116},{24,16},{28,124},{32... | collective-permute-start | bytes 5505032 | tf_op jit(solution)/shard_map/ppermute | solution.py:119
  35.3 0.0 collective-permute-done.8
  35.3 3.4 %add_convert_fusion = bf16[3,448,512]{2,1,0:T(8,128)(2,1)} fusion(bf16[4,448,512]{2,1,0:T(8,128)(2,1)} %collective-permute-done.8, bf16[4,448,512]{2,1,0:T(8,128)(2,1)} %get-tuple-element.43), kind=kLoop, calls=%fused_computation | loop fusion | flops 2752512 | bytes 4128768 | tf_op jit(solution)/shard_map/convert_element_type | solution.py:167
  38.8 0.3 collective-permute-start.10
  39.1 0.0 collective-permute-done.2
  39.1 1.5 %add_convert_fusion.1 = bf16[3,448,512]{2,1,0:T(8,128)(2,1)} fusion(bf16[4,448,512]{2,1,0:T(8,128)(2,1)S(1)} %collective-permute-done.2, bf16[4,448,512]{2,1,0:T(8,128)(2,1)S(1)} %copy-done.2), kind=kLoop, calls=%fused_computation.1 | loop fusion | flops 2752512 | bytes 4128768 | tf_op jit(solution)/shard_map/convert_element_type | solution.py:167
  40.6 2.9 %collective-permute-start.4 = (bf16[3,448,512]{2,1,0:T(8,128)(2,1)}, bf16[3,448,512]{2,1,0:T(8,128)(2,1)}, u32[]{:S(2)}, u32[]{:S(2)}) collective-permute-start(bf16[3,448,512]{2,1,0:T(8,128)(2,1)} %add_convert_fusion.1), channel_id=1, source_target_pairs={{0,24},{4,100},{8,0},{12,108},{16,8},{20,116},{24,16},{28,124},{32... | collective-permute-start | bytes 4128776 | tf_op jit(solution)/shard_map/ppermute | solution.py:119
  43.5 2.0 %fusion.1 = bf16[448,512]{1,0:T(8,128)(2,1)} fusion(bf16[4,448,512]{2,1,0:T(8,128)(2,1)} %collective-permute-done.8, bf16[4,448,512]{2,1,0:T(8,128)(2,1)} %get-tuple-element.43), kind=kLoop, calls=%fused_computation.5 | loop fusion | flops 917504 | bytes 1376256 | tf_op jit(solution)/shard_map/convert_element_type | solution.py:167
  45.6 0.0 collective-permute-start.9
  45.6 9.3 %collective-permute-done.1.refs_1_ = bf16[4,448,512]{2,1,0:T(8,128)(2,1)S(1)} collective-permute-done((bf16[4,448,512]{2,1,0:T(8,128)(2,1)}, bf16[4,448,512]{2,1,0:T(8,128)(2,1)S(1)}, u32[]{:S(2)}, u32[]{:S(2)}) %collective-permute-start.1) | collective-permute-done | bytes 1835040 | tf_op jit(solution)/shard_map/ppermute | solution.py:119
  54.8 1.6 %collective-permute-done.refs_0_ = bf16[4,448,512]{2,1,0:T(8,128)(2,1)S(1)} collective-permute-done((bf16[4,448,512]{2,1,0:T(8,128)(2,1)}, bf16[4,448,512]{2,1,0:T(8,128)(2,1)S(1)}, u32[]{:S(2)}, u32[]{:S(2)}) %collective-permute-start) | collective-permute-done | bytes 1835040 | tf_op jit(solution)/shard_map/ppermute | solution.py:119
  56.4 1.2 copy-done.1
  57.6 10.4 %shard_map.120 = (bf16[4,448,512]{2,1,0:T(8,128)(2,1)}, bf16[4,448,512]{2,1,0:T(8,128)(2,1)}) custom-call(s32[32]{0:T(128)} %pad_add_fusion.where, bf16[1024,7168]{1,0:T(8,128)(2,1)} %hidden.7, bf16[1024,1024]{1,0:T(8,128)(2,1)} %upstream.7, bf16[4,448,512]{2,1,0:T(8,128)(2,1)} %copy-done.1, bf16[4,448,512]{2,1,0:T(8,128)(2,1)} %copy-done), custom_call_target="tpu_custom_call" | custom-call | flops 3758096384 | bytes 10485760 | tf_op jit(solution)/shard_map/pallas_call | solution.py:75
  68.0 1.7 %collective-permute-done.10.got = bf16[3,448,512]{2,1,0:T(8,128)(2,1)} collective-permute-done((bf16[3,448,512]{2,1,0:T(8,128)(2,1)}, bf16[3,448,512]{2,1,0:T(8,128)(2,1)}, u32[]{:S(2)}, u32[]{:S(2)}) %collective-permute-start.10) | collective-permute-done | bytes 1376288 | tf_op jit(solution)/shard_map/ppermute | solution.py:119
  69.7 2.7 %shard_map.123 = (bf16[448,512]{1,0:T(8,128)(2,1)}, bf16[448,512]{1,0:T(8,128)(2,1)}, bf16[448,512]{1,0:T(8,128)(2,1)}) custom-call(bf16[4,448,512]{2,1,0:T(8,128)(2,1)} %get-tuple-element.42.kept.own, bf16[3,448,512]{2,1,0:T(8,128)(2,1)} %collective-permute-done.10.got), custom_call_target="tpu_custom_call" | custom-call | flops 688128 | bytes 4194304 | tf_op jit(solution)/shard_map/pallas_call | solution.py:148
  72.3 3.4 %collective-permute-start.11 = (bf16[448,512]{1,0:T(8,128)(2,1)}, bf16[448,512]{1,0:T(8,128)(2,1)S(1)}, u32[]{:S(2)}, u32[]{:S(2)}) collective-permute-start(bf16[448,512]{1,0:T(8,128)(2,1)} %get-tuple-element.45), channel_id=1, source_target_pairs={{0,64},{4,20},{8,72},{12,28},{16,80},{20,4},{24,88},{28,12},{32,96... | collective-permute-start | bytes 1376264 | tf_op jit(solution)/shard_map/ppermute | solution.py:119
  75.7 0.7 collective-permute-start.12
  76.4 2.6 %collective-permute-start.13 = (bf16[448,512]{1,0:T(8,128)(2,1)}, bf16[448,512]{1,0:T(8,128)(2,1)S(1)}, u32[]{:S(2)}, u32[]{:S(2)}) collective-permute-start(bf16[448,512]{1,0:T(8,128)(2,1)} %get-tuple-element.47), channel_id=1, source_target_pairs={{0,96},{4,28},{8,104},{12,4},{16,112},{20,12},{24,120},{28,20},{32... | collective-permute-start | bytes 1376264 | tf_op jit(solution)/shard_map/ppermute | solution.py:119
  79.0 1.1 fusion
  80.1 0.0 copy-start.10
  80.1 1.9 %collective-permute-start.3 = (bf16[448,512]{1,0:T(8,128)(2,1)S(1)}, bf16[448,512]{1,0:T(8,128)(2,1)S(1)}, u32[]{:S(2)}, u32[]{:S(2)}) collective-permute-start(bf16[448,512]{1,0:T(8,128)(2,1)S(1)} %fusion), channel_id=1, source_target_pairs={{0,24},{4,100},{8,0},{12,108},{16,8},{20,116},{24,16},{28,124},{32... | collective-permute-start | bytes 1376264 | tf_op jit(solution)/shard_map/ppermute | solution.py:119
  82.1 2.7 %shard_map.122 = (bf16[448,512]{1,0:T(8,128)(2,1)}, bf16[448,512]{1,0:T(8,128)(2,1)}, bf16[448,512]{1,0:T(8,128)(2,1)}) custom-call(bf16[4,448,512]{2,1,0:T(8,128)(2,1)} %get-tuple-element.36.kept.own, bf16[3,448,512]{2,1,0:T(8,128)(2,1)} %collective-permute-done.4.got), custom_call_target="tpu_custom_call" | custom-call | flops 688128 | bytes 4194304 | tf_op jit(solution)/shard_map/pallas_call | solution.py:148
  84.8 0.0 collective-permute-done.9.added
  84.8 0.0 copy-start.3
  84.8 0.1 collective-permute-start.5
  84.9 1.7 %collective-permute-start.6 = (bf16[448,512]{1,0:T(8,128)(2,1)}, bf16[448,512]{1,0:T(8,128)(2,1)}, u32[]{:S(2)}, u32[]{:S(2)}) collective-permute-start(bf16[448,512]{1,0:T(8,128)(2,1)} %get-tuple-element.40), channel_id=1, source_target_pairs={{0,32},{4,12},{8,40},{12,20},{16,48},{20,28},{24,56},{28,4},{32,64... | collective-permute-start | bytes 1376264 | tf_op jit(solution)/shard_map/ppermute | solution.py:119
  86.6 1.0 collective-permute-done.12.up
  87.5 0.8 collective-permute-start.7
  88.4 0.9 copy.19.rows
  89.2 8.0 %collective-permute-done.13.down = bf16[448,512]{1,0:T(8,128)(2,1)S(1)} collective-permute-done((bf16[448,512]{1,0:T(8,128)(2,1)}, bf16[448,512]{1,0:T(8,128)(2,1)S(1)}, u32[]{:S(2)}, u32[]{:S(2)}) %collective-permute-start.13) | collective-permute-done | bytes 458784 | tf_op jit(solution)/shard_map/ppermute | solution.py:119
  97.2 0.8 copy-done.6
  98.0 3.9 %shard_map.124 = (f32[448,512]{1,0:T(8,128)}, f32[448,512]{1,0:T(8,128)}, f32[1,448]{1,0:T(1,128)}, f32[1,512]{1,0:T(1,128)}) custom-call(bf16[4,448,512]{2,1,0:T(8,128)(2,1)} %get-tuple-element.42.kept.own, bf16[448,512]{1,0:T(8,128)(2,1)} %copy-done.3, bf16[448,512]{1,0:T(8,128)(2,1)} %copy-done.4, bf16[448,512]{1,0:T(8,128)(2,1)} %copy-done.5, ...), custom_call_target="tpu_custom_call" | custom-call | flops 4587520 | bytes 5242880 | tf_op jit(solution)/shard_map/pallas_call | solution.py:264
  101.9 0.0 copy-start.7
  101.9 0.0 copy-start.8
  101.9 1.0 collective-permute-done.7.down
  102.9 4.6 %shard_map.125 = (f32[448,512]{1,0:T(8,128)}, f32[448,512]{1,0:T(8,128)}, f32[1,448]{1,0:T(1,128)}, f32[1,1024]{1,0:T(1,128)}) custom-call(bf16[4,448,512]{2,1,0:T(8,128)(2,1)} %get-tuple-element.36.kept.own, bf16[448,512]{1,0:T(8,128)(2,1)} %copy-done.7, bf16[448,512]{1,0:T(8,128)(2,1)} %copy-done.8, bf16[448,512]{1,0:T(8,128)(2,1)} %collective-permute-done.6.up, ...), custom_call_target="tpu_custom_call" | custom-call | flops 4587520 | bytes 5242880 | tf_op jit(solution)/shard_map/pallas_call | solution.py:264
  107.4 0.1 collective-permute-start.16
  107.5 1.4 collective-permute-done.16
  108.9 0.7 max.29
  109.6 1.9 %collective-permute-start.19 = (f32[1,1024]{1,0:T(1,128)S(1)}, f32[1,1024]{1,0:T(1,128)S(1)}, u32[]{:S(2)}, u32[]{:S(2)}) collective-permute-start(f32[1,1024]{1,0:T(1,128)S(1)} %max.29), channel_id=1, source_target_pairs={{0,24},{4,100},{8,0},{12,108},{16,8},{20,116},{24,16},{28,124},{32... | collective-permute-start | bytes 12296 | tf_op jit(solution)/shard_map/ppermute | solution.py:362
  111.5 0.5 collective-permute-start.18
  112.0 0.9 collective-permute-start.17
  112.8 1.9 %collective-permute-start.14 = (f32[1,448]{1,0:T(1,128)}, f32[1,448]{1,0:T(1,128)S(1)}, u32[]{:S(2)}, u32[]{:S(2)}) collective-permute-start(f32[1,448]{1,0:T(1,128)} %get-tuple-element.60), channel_id=1, source_target_pairs={{0,1},{1,0},{2,3},{3,2},{4,5},{5,4},{6,7},{7,6},{8,9},{9,8},{10,11... | collective-permute-start | bytes 5384 | tf_op jit(solution)/shard_map/ppermute | solution.py:390
  114.8 1.8 %collective-permute-done.18 = f32[1,1024]{1,0:T(1,128)S(1)} collective-permute-done((f32[1,1024]{1,0:T(1,128)S(1)}, f32[1,1024]{1,0:T(1,128)S(1)}, u32[]{:S(2)}, u32[]{:S(2)}) %collective-permute-start.18) | collective-permute-done | bytes 4128 | tf_op jit(solution)/shard_map/ppermute | solution.py:362
  116.6 0.2 collective-permute-done.17
  116.8 3.4 %collective-permute-start.22 = (f32[1,1024]{1,0:T(1,128)S(1)}, f32[1,1024]{1,0:T(1,128)S(1)}, u32[]{:S(2)}, u32[]{:S(2)}) collective-permute-start(f32[1,1024]{1,0:T(1,128)S(1)} %maximum_maximum_fusion.1), channel_id=1, source_target_pairs={{0,96},{4,28},{8,104},{12,4},{16,112},{20,12},{24,120},{28,20},{32... | collective-permute-start | bytes 12296 | tf_op jit(solution)/shard_map/ppermute | solution.py:362
  120.2 0.9 collective-permute-start.20
  121.1 0.8 copy.21.scale
  121.9 0.7 max.27
  122.6 3.9 %collective-permute-start.15 = (f32[1,448]{1,0:T(1,128)S(1)}, f32[1,448]{1,0:T(1,128)S(1)}, u32[]{:S(2)}, u32[]{:S(2)}) collective-permute-start(f32[1,448]{1,0:T(1,128)S(1)} %max.27), channel_id=1, source_target_pairs={{0,2},{1,3},{2,0},{3,1},{4,6},{5,7},{6,4},{7,5},{8,10},{9,11},{10,... | collective-permute-start | bytes 5384 | tf_op jit(solution)/shard_map/ppermute | solution.py:390
  126.5 4.4 %shard_map.126 = (f32[448,1024]{1,0:T(8,128)}, bf16[448,1024]{1,0:T(8,128)(2,1)}, f32[448,8]{1,0:T(8,128)}) custom-call(f32[448,512]{1,0:T(8,128)} %get-tuple-element.52.gradient, f32[448,512]{1,0:T(8,128)} %get-tuple-element.53.second.low, s32[448,1024]{1,0:T(8,128)} %codes.7, f32[448,8]{1,0:T(8,128)} %copy.21.scale), custom_call_target="tpu_custom_call" | custom-call | flops 9175040 | bytes 5242880 | tf_op jit(solution)/shard_map/pallas_call | solution.py:320
  130.9 4.4 %shard_map.127 = (f32[448,1024]{1,0:T(8,128)}, bf16[448,1024]{1,0:T(8,128)(2,1)}, f32[448,8]{1,0:T(8,128)}) custom-call(f32[448,512]{1,0:T(8,128)} %get-tuple-element.50.gradient, f32[448,512]{1,0:T(8,128)} %get-tuple-element.51.second.high, s32[448,1024]{1,0:T(8,128)} %codes.7, f32[448,8]{1,0:T(8,128)} %copy.21.scale, ...), custom_call_target="tpu_custom_call", output_to_operand_aliasing={{0}: (5, {}), {1}: (6, {})} | custom-call | flops 9175040 | bytes 5242880 | tf_op jit(solution)/shard_map/pallas_call | solution.py:320
  135.3 1.6 %copy.22 = f32[448,8]{0,1:T(8,128)} copy(f32[448,8]{1,0:T(8,128)} %get-tuple-element.70) | data formatting | bytes 28672
  137.0 0.6 max.28.row_peak
  137.6 0.6 maximum_maximum_fusion.column_peak
  138.2 2.8 %norm.1 = bf16[448,1024]{1,0:T(8,128)(2,1)} custom-call(f32[448,512]{1,0:T(8,128)} %get-tuple-element.53.second.low, f32[448,512]{1,0:T(8,128)} %get-tuple-element.51.second.high, f32[1,448]{1,0:T(1,128)} %max.28.row_peak, f32[1,1024]{1,0:T(1,128)} %maximum_maximum_fusion.column_peak), custom_call_target="tpu_custom_call" | custom-call | tf_op jit(solution)/shard_map/norm/pallas_call | solution.py:351
  (30 shorter events, 0.1 us)
Async XLA Ops:
  10.4 24.9 %collective-permute-start.8 = (bf16[4,448,512]{2,1,0:T(8,128)(2,1)}, bf16[4,448,512]{2,1,0:T(8,128)(2,1)}, u32[]{:S(2)}, u32[]{:S(2)}) collective-permute-start(bf16[4,448,512]{2,1,0:T(8,128)(2,1)} %get-tuple-element.44), channel_id=1, source_target_pairs={{0,8},{4,36},{8,16},{12,44},{16,24},{20,52},{24,0},{28,60},{32,40}... | collective-permute-start | bytes 5505032 | tf_op jit(solution)/shard_map/ppermute | solution.py:119
  12.1 27.0 %collective-permute-start.2 = (bf16[4,448,512]{2,1,0:T(8,128)(2,1)}, bf16[4,448,512]{2,1,0:T(8,128)(2,1)S(1)}, u32[]{:S(2)}, u32[]{:S(2)}) collective-permute-start(bf16[4,448,512]{2,1,0:T(8,128)(2,1)} %get-tuple-element.38), channel_id=1, source_target_pairs={{0,24},{4,100},{8,0},{12,108},{16,8},{20,116},{24,16},{28,124},{32... | collective-permute-start | bytes 5505032 | tf_op jit(solution)/shard_map/ppermute | solution.py:119
  22.8 32.1 %collective-permute-start.1 = (bf16[4,448,512]{2,1,0:T(8,128)(2,1)}, bf16[4,448,512]{2,1,0:T(8,128)(2,1)S(1)}, u32[]{:S(2)}, u32[]{:S(2)}) collective-permute-start(bf16[4,448,512]{2,1,0:T(8,128)(2,1)} %get-tuple-element.35), channel_id=1, source_target_pairs={{0,8},{4,36},{8,16},{12,44},{16,24},{20,52},{24,0},{28,60},{32,40}... | collective-permute-start | bytes 5505032 | tf_op jit(solution)/shard_map/ppermute | solution.py:119
  32.4 24.0 %collective-permute-start = (bf16[4,448,512]{2,1,0:T(8,128)(2,1)}, bf16[4,448,512]{2,1,0:T(8,128)(2,1)S(1)}, u32[]{:S(2)}, u32[]{:S(2)}) collective-permute-start(bf16[4,448,512]{2,1,0:T(8,128)(2,1)} %get-tuple-element.34), channel_id=1, source_target_pairs={{0,24},{4,100},{8,0},{12,108},{16,8},{20,116},{24,16},{28,124},{32... | collective-permute-start | bytes 5505032 | tf_op jit(solution)/shard_map/ppermute | solution.py:119
  35.3 3.8 %copy-start.2 = (bf16[4,448,512]{2,1,0:T(8,128)(2,1)S(1)}, bf16[4,448,512]{2,1,0:T(8,128)(2,1)}, u32[]{:S(2)}) copy-start(bf16[4,448,512]{2,1,0:T(8,128)(2,1)} %get-tuple-element.37) | copy-start | bytes 5505028
  38.8 30.9 %collective-permute-start.10 = (bf16[3,448,512]{2,1,0:T(8,128)(2,1)}, bf16[3,448,512]{2,1,0:T(8,128)(2,1)}, u32[]{:S(2)}, u32[]{:S(2)}) collective-permute-start(bf16[3,448,512]{2,1,0:T(8,128)(2,1)} %add_convert_fusion), channel_id=1, source_target_pairs={{0,8},{4,36},{8,16},{12,44},{16,24},{20,52},{24,0},{28,60},{32,40}... | collective-permute-start | bytes 4128776 | tf_op jit(solution)/shard_map/ppermute | solution.py:119
  40.6 39.5 %collective-permute-start.4 = (bf16[3,448,512]{2,1,0:T(8,128)(2,1)}, bf16[3,448,512]{2,1,0:T(8,128)(2,1)}, u32[]{:S(2)}, u32[]{:S(2)}) collective-permute-start(bf16[3,448,512]{2,1,0:T(8,128)(2,1)} %add_convert_fusion.1), channel_id=1, source_target_pairs={{0,24},{4,100},{8,0},{12,108},{16,8},{20,116},{24,16},{28,124},{32... | collective-permute-start | bytes 4128776 | tf_op jit(solution)/shard_map/ppermute | solution.py:119
  45.6 39.2 %collective-permute-start.9 = (bf16[448,512]{1,0:T(8,128)(2,1)}, bf16[448,512]{1,0:T(8,128)(2,1)S(1)}, u32[]{:S(2)}, u32[]{:S(2)}) collective-permute-start(bf16[448,512]{1,0:T(8,128)(2,1)} %fusion.1), channel_id=1, source_target_pairs={{0,8},{4,36},{8,16},{12,44},{16,24},{20,52},{24,0},{28,60},{32,40}... | collective-permute-start | bytes 1376264 | tf_op jit(solution)/shard_map/ppermute | solution.py:119
  54.8 1.6 %copy-start = (bf16[4,448,512]{2,1,0:T(8,128)(2,1)}, bf16[4,448,512]{2,1,0:T(8,128)(2,1)S(1)}, u32[]{:S(2)}) copy-start(bf16[4,448,512]{2,1,0:T(8,128)(2,1)S(1)} %collective-permute-done.1.refs_1_) | copy-start | bytes 5505028
  56.4 1.2 copy-start.1
  72.3 12.5 %collective-permute-start.11 = (bf16[448,512]{1,0:T(8,128)(2,1)}, bf16[448,512]{1,0:T(8,128)(2,1)S(1)}, u32[]{:S(2)}, u32[]{:S(2)}) collective-permute-start(bf16[448,512]{1,0:T(8,128)(2,1)} %get-tuple-element.45), channel_id=1, source_target_pairs={{0,64},{4,20},{8,72},{12,28},{16,80},{20,4},{24,88},{28,12},{32,96... | collective-permute-start | bytes 1376264 | tf_op jit(solution)/shard_map/ppermute | solution.py:119
  75.7 11.8 %collective-permute-start.12 = (bf16[448,512]{1,0:T(8,128)(2,1)}, bf16[448,512]{1,0:T(8,128)(2,1)S(1)}, u32[]{:S(2)}, u32[]{:S(2)}) collective-permute-start(bf16[448,512]{1,0:T(8,128)(2,1)} %get-tuple-element.46), channel_id=1, source_target_pairs={{0,32},{4,12},{8,40},{12,20},{16,48},{20,28},{24,56},{28,4},{32,64... | collective-permute-start | bytes 1376264 | tf_op jit(solution)/shard_map/ppermute | solution.py:119
  76.4 20.8 %collective-permute-start.13 = (bf16[448,512]{1,0:T(8,128)(2,1)}, bf16[448,512]{1,0:T(8,128)(2,1)S(1)}, u32[]{:S(2)}, u32[]{:S(2)}) collective-permute-start(bf16[448,512]{1,0:T(8,128)(2,1)} %get-tuple-element.47), channel_id=1, source_target_pairs={{0,96},{4,28},{8,104},{12,4},{16,112},{20,12},{24,120},{28,20},{32... | collective-permute-start | bytes 1376264 | tf_op jit(solution)/shard_map/ppermute | solution.py:119
  80.1 8.3 %copy-start.10 = (f32[448]{0:T(512)S(1)}, f32[448]{0:T(512)}, u32[]{:S(2)}) copy-start(f32[448]{0:T(512)} %param.12) | copy-start | bytes 5380
  80.1 21.7 %collective-permute-start.3 = (bf16[448,512]{1,0:T(8,128)(2,1)S(1)}, bf16[448,512]{1,0:T(8,128)(2,1)S(1)}, u32[]{:S(2)}, u32[]{:S(2)}) collective-permute-start(bf16[448,512]{1,0:T(8,128)(2,1)S(1)} %fusion), channel_id=1, source_target_pairs={{0,24},{4,100},{8,0},{12,108},{16,8},{20,116},{24,16},{28,124},{32... | collective-permute-start | bytes 1376264 | tf_op jit(solution)/shard_map/ppermute | solution.py:119
  84.8 12.4 %copy-start.3 = (bf16[448,512]{1,0:T(8,128)(2,1)}, bf16[448,512]{1,0:T(8,128)(2,1)S(1)}, u32[]{:S(2)}) copy-start(bf16[448,512]{1,0:T(8,128)(2,1)S(1)} %collective-permute-done.9.added) | copy-start | bytes 1376260
  84.8 17.1 %collective-permute-start.5 = (bf16[448,512]{1,0:T(8,128)(2,1)}, bf16[448,512]{1,0:T(8,128)(2,1)S(1)}, u32[]{:S(2)}, u32[]{:S(2)}) collective-permute-start(bf16[448,512]{1,0:T(8,128)(2,1)} %get-tuple-element.39), channel_id=1, source_target_pairs={{0,64},{4,20},{8,72},{12,28},{16,80},{20,4},{24,88},{28,12},{32,96... | collective-permute-start | bytes 1376264 | tf_op jit(solution)/shard_map/ppermute | solution.py:119
  84.9 12.3 %copy-start.4 = (bf16[448,512]{1,0:T(8,128)(2,1)}, bf16[448,512]{1,0:T(8,128)(2,1)S(1)}, u32[]{:S(2)}) copy-start(bf16[448,512]{1,0:T(8,128)(2,1)S(1)} %collective-permute-done.11.far) | copy-start | bytes 1376260
  84.9 17.0 %collective-permute-start.6 = (bf16[448,512]{1,0:T(8,128)(2,1)}, bf16[448,512]{1,0:T(8,128)(2,1)}, u32[]{:S(2)}, u32[]{:S(2)}) collective-permute-start(bf16[448,512]{1,0:T(8,128)(2,1)} %get-tuple-element.40), channel_id=1, source_target_pairs={{0,32},{4,12},{8,40},{12,20},{16,48},{20,28},{24,56},{28,4},{32,64... | collective-permute-start | bytes 1376264 | tf_op jit(solution)/shard_map/ppermute | solution.py:119
  87.5 9.7 %copy-start.5 = (bf16[448,512]{1,0:T(8,128)(2,1)}, bf16[448,512]{1,0:T(8,128)(2,1)S(1)}, u32[]{:S(2)}) copy-start(bf16[448,512]{1,0:T(8,128)(2,1)S(1)} %collective-permute-done.12.up) | copy-start | bytes 1376260
  87.5 15.3 %collective-permute-start.7 = (bf16[448,512]{1,0:T(8,128)(2,1)}, bf16[448,512]{1,0:T(8,128)(2,1)}, u32[]{:S(2)}, u32[]{:S(2)}) collective-permute-start(bf16[448,512]{1,0:T(8,128)(2,1)} %get-tuple-element.41), channel_id=1, source_target_pairs={{0,96},{4,28},{8,104},{12,4},{16,112},{20,12},{24,120},{28,20},{32... | collective-permute-start | bytes 1376264 | tf_op jit(solution)/shard_map/ppermute | solution.py:119
  97.2 0.8 copy-start.6
  101.9 1.0 copy-start.7
  101.9 1.0 copy-start.8
  102.9 18.2 %copy-start.9 = (f32[448,8]{0,1:T(8,128)S(1)}, f32[448,8]{0,1:T(8,128)}, u32[]{:S(2)}) copy-start(f32[448,8]{0,1:T(8,128)} %param.10) | copy-start | bytes 43012
  107.4 1.5 %collective-permute-start.16 = (f32[1,1024]{1,0:T(1,128)}, f32[1,1024]{1,0:T(1,128)S(1)}, u32[]{:S(2)}, u32[]{:S(2)}) collective-permute-start(f32[1,1024]{1,0:T(1,128)} %get-tuple-element.61), channel_id=1, source_target_pairs={{0,4},{4,0},{1,5},{5,1},{2,6},{6,2},{3,7},{7,3},{8,12},{12,8},{9,1... | collective-permute-start | bytes 12296 | tf_op jit(solution)/shard_map/ppermute | solution.py:388
  109.6 5.2 %collective-permute-start.19 = (f32[1,1024]{1,0:T(1,128)S(1)}, f32[1,1024]{1,0:T(1,128)S(1)}, u32[]{:S(2)}, u32[]{:S(2)}) collective-permute-start(f32[1,1024]{1,0:T(1,128)S(1)} %max.29), channel_id=1, source_target_pairs={{0,24},{4,100},{8,0},{12,108},{16,8},{20,116},{24,16},{28,124},{32... | collective-permute-start | bytes 12296 | tf_op jit(solution)/shard_map/ppermute | solution.py:362
  111.5 5.1 %collective-permute-start.18 = (f32[1,1024]{1,0:T(1,128)S(1)}, f32[1,1024]{1,0:T(1,128)S(1)}, u32[]{:S(2)}, u32[]{:S(2)}) collective-permute-start(f32[1,1024]{1,0:T(1,128)S(1)} %max.29), channel_id=1, source_target_pairs={{0,16},{4,68},{8,24},{12,76},{16,0},{20,84},{24,8},{28,92},{32,48}... | collective-permute-start | bytes 12296 | tf_op jit(solution)/shard_map/ppermute | solution.py:362
  112.0 4.8 %collective-permute-start.17 = (f32[1,1024]{1,0:T(1,128)S(1)}, f32[1,1024]{1,0:T(1,128)S(1)}, u32[]{:S(2)}, u32[]{:S(2)}) collective-permute-start(f32[1,1024]{1,0:T(1,128)S(1)} %max.29), channel_id=1, source_target_pairs={{0,8},{4,36},{8,16},{12,44},{16,24},{20,52},{24,0},{28,60},{32,40}... | collective-permute-start | bytes 12296 | tf_op jit(solution)/shard_map/ppermute | solution.py:362
  112.8 9.1 %collective-permute-start.14 = (f32[1,448]{1,0:T(1,128)}, f32[1,448]{1,0:T(1,128)S(1)}, u32[]{:S(2)}, u32[]{:S(2)}) collective-permute-start(f32[1,448]{1,0:T(1,128)} %get-tuple-element.60), channel_id=1, source_target_pairs={{0,1},{1,0},{2,3},{3,2},{4,5},{5,4},{6,7},{7,6},{8,9},{9,8},{10,11... | collective-permute-start | bytes 5384 | tf_op jit(solution)/shard_map/ppermute | solution.py:390
  116.8 20.8 %collective-permute-start.22 = (f32[1,1024]{1,0:T(1,128)S(1)}, f32[1,1024]{1,0:T(1,128)S(1)}, u32[]{:S(2)}, u32[]{:S(2)}) collective-permute-start(f32[1,1024]{1,0:T(1,128)S(1)} %maximum_maximum_fusion.1), channel_id=1, source_target_pairs={{0,96},{4,28},{8,104},{12,4},{16,112},{20,12},{24,120},{28,20},{32... | collective-permute-start | bytes 12296 | tf_op jit(solution)/shard_map/ppermute | solution.py:362
  120.2 17.4 %collective-permute-start.21 = (f32[1,1024]{1,0:T(1,128)S(1)}, f32[1,1024]{1,0:T(1,128)S(1)}, u32[]{:S(2)}, u32[]{:S(2)}) collective-permute-start(f32[1,1024]{1,0:T(1,128)S(1)} %maximum_maximum_fusion.1), channel_id=1, source_target_pairs={{0,64},{4,20},{8,72},{12,28},{16,80},{20,4},{24,88},{28,12},{32,96... | collective-permute-start | bytes 12296 | tf_op jit(solution)/shard_map/ppermute | solution.py:362
  120.2 17.4 %collective-permute-start.20 = (f32[1,1024]{1,0:T(1,128)S(1)}, f32[1,1024]{1,0:T(1,128)S(1)}, u32[]{:S(2)}, u32[]{:S(2)}) collective-permute-start(f32[1,1024]{1,0:T(1,128)S(1)} %maximum_maximum_fusion.1), channel_id=1, source_target_pairs={{0,32},{4,12},{8,40},{12,20},{16,48},{20,28},{24,56},{28,4},{32,64... | collective-permute-start | bytes 12296 | tf_op jit(solution)/shard_map/ppermute | solution.py:362
  122.6 14.4 %collective-permute-start.15 = (f32[1,448]{1,0:T(1,128)S(1)}, f32[1,448]{1,0:T(1,128)S(1)}, u32[]{:S(2)}, u32[]{:S(2)}) collective-permute-start(f32[1,448]{1,0:T(1,128)S(1)} %max.27), channel_id=1, source_target_pairs={{0,2},{1,3},{2,0},{3,1},{4,6},{5,7},{6,4},{7,5},{8,10},{9,11},{10,... | collective-permute-start | bytes 5384 | tf_op jit(solution)/shard_map/ppermute | solution.py:390

commit v2 on v1

--- a/solution.py
+++ b/solution.py
@@ -20,7 +20,12 @@
 ANY = pl.BlockSpec(memory_space=pl.ANY)
 
 
+SMALL = pltpu.CompilerParams(vmem_limit_bytes=16 << 20)
 GRANT = pltpu.CompilerParams(vmem_limit_bytes=58 << 20)
+
+
+def in_hbm(a):
+    return pltpu.with_memory_space_constraint(a, pltpu.MemorySpace.HBM)
 
 
 def dot(left, right):
@@ -158,7 +163,7 @@
         cost_estimate=pl.CostEstimate(
             flops=3 * OWN * HALF, bytes_accessed=4 << 20, transcendentals=0
         ),
-        compiler_params=GRANT,
+        compiler_params=SMALL,
     )(kept, got)
     return (send(far, other(2)), send(up, other(1)), send(down, other(-1)))
 
@@ -182,9 +187,10 @@
     added_low_own = send(add(up_low[3], from_low[3]), near(1))
     added_high_own = send(add(down_high[3], from_high[3]), near(-1))
     own_low, own_high = product(hidden, upstream, where, 12, (direct_low, direct_high))
+    kept_low, kept_high = in_hbm(own_low), in_hbm(own_high)
     return (
-        (own_low, added_low_own, *last(own_low, added_low)),
-        (own_high, added_high_own, *last(own_high, added_high)),
+        (own_low[3].astype(F32) + added_low_own.astype(F32), *last(kept_low, added_low)),
+        (own_high[3].astype(F32) + added_high_own.astype(F32), *last(kept_high, added_high)),
     )
 
 
@@ -192,75 +198,49 @@
 CHUNKS = OWN // TALL
 
 
-def second_kernel(half, own, added, far, up, down, codes, rows, columns, *refs):
+def second_kernel(half, own, far, up, down, codes, rows, columns, *refs):
     before, refs = (refs[:2], refs[2:]) if half else ((), refs)
-    gradient, second, row_out, column_out = refs[:4]
-    parts, code, row, column, made, wide, sems = refs[4:]
-    here = pl.ds(half * HALF, HALF)
-    small = [
-        pltpu.make_async_copy(rows, row, sems.at[0]),
-        pltpu.make_async_copy(columns.at[:, here], column, sems.at[1]),
-    ]
-    loads = []
-    for i in range(CHUNKS):
-        at = pl.ds(i * TALL, TALL)
-        sources = [own.at[3, at], added.at[at], far.at[at], up.at[at], down.at[at]]
-        group = [
-            pltpu.make_async_copy(a, parts.at[n, at], sems.at[2 + 6 * i + n])
-            for n, a in enumerate(sources)
-        ]
-        group.append(
-            pltpu.make_async_copy(codes.at[at, here], code.at[at], sems.at[2 + 6 * i + 5])
-        )
-        loads.append(group)
-    for copy in small:
-        copy.start()
-    for group in loads:
-        for copy in group:
-            copy.start()
-    for copy in small:
-        copy.wait()
-    peak = None
-    stores = []
-    for i in range(CHUNKS):
-        at = pl.ds(i * TALL, TALL)
-        for copy in loads[i]:
-            copy.wait()
-        total = parts[0, at, :].astype(F32)
-        for n in range(1, 5):
-            total = total + parts[n, at, :].astype(F32)
-        level = (code[at, :].astype(F32) + 1.0) / 16.0
-        old = jnp.minimum(row[at, :], column[...]) * level
-        new = 0.999 * old + 0.001 * total * total
-        made[0, at, :] = total
-        made[1, at, :] = new
-        for n, out in enumerate((gradient, second)):
-            copy = pltpu.make_async_copy(
-                made.at[n, at], out.at[at], sems.at[2 + 6 * CHUNKS + 2 * i + n]
-            )
-            copy.start()
-            stores.append(copy)
-        top = jnp.max(new, axis=0, keepdims=True)
-        peak = top if peak is None else jnp.maximum(peak, top)
-        widest = new[:, :LANES]
-        for b in range(1, HALF // LANES):
-            widest = jnp.maximum(widest, new[:, b * LANES : (b + 1) * LANES])
-        wide[at, :] = widest
-    row_top = jnp.max(wide[...].T, axis=0, keepdims=True)
-    if half:
-        row_out[...] = jnp.maximum(row_top, before[0][...])
-        column_out[:, :HALF] = before[1][...]
-        column_out[:, HALF:] = peak
-    else:
-        row_out[...] = row_top
-        column_out[...] = peak
-    for copy in stores:
-        copy.wait()
+    gradient, second, row_out, column_out, wide = refs
+    i = pl.program_id(0)
+    total = own[...]
+    for ref in (far, up, down):
+        total = total + ref[...].astype(F32)
+    level = (codes[...].astype(F32) + 1.0) / 16.0
+    old = jnp.minimum(rows[...], columns[...]) * level
+    new = 0.999 * old + 0.001 * total * total
+    gradient[...] = total
+    second[...] = new
+    peak = jnp.max(new, axis=0, keepdims=True)
+    here = slice(half * HALF, (half + 1) * HALF)
+
+    @pl.when(i == 0)
+    def _():
+        column_out[:, here] = peak
+        if half:
+            column_out[:, :HALF] = before[1][...]
+
+    @pl.when(i > 0)
+    def _():
+        column_out[:, here] = jnp.maximum(column_out[:, here], peak)
+
+    widest = new[:, :LANES]
+    for b in range(1, HALF // LANES):
+        widest = jnp.maximum(widest, new[:, b * LANES : (b + 1) * LANES])
+    wide[pl.ds(pl.multiple_of(i * TALL, TALL), TALL), :] = widest
+
+    @pl.when(i == pl.num_programs(0) - 1)
+    def _():
+        row_top = jnp.max(wide[...].T, axis=0, keepdims=True)
+        row_out[...] = jnp.maximum(row_top, before[0][...]) if half else row_top
 
 
 def second_moment(half, parts, codes, rows, columns, before=()):
-    vmem = pl.BlockSpec(memory_space=pltpu.MemorySpace.VMEM)
     reach = HALF * (1 + half)
+    half_spec = pl.BlockSpec((TALL, HALF), lambda i: (i, 0))
+
+    def whole(width):
+        return pl.BlockSpec((1, width), lambda i: (0, 0))
+
     return pl.pallas_call(
         functools.partial(second_kernel, half),
         out_shape=(
@@ -269,26 +249,25 @@
             jax.ShapeDtypeStruct((1, OWN), F32),
             jax.ShapeDtypeStruct((1, reach), F32),
         ),
-        in_specs=[ANY] * 8 + [vmem] * len(before),
-        out_specs=(ANY, ANY, vmem, vmem),
-        scratch_shapes=[
-            pltpu.VMEM((5, OWN, HALF), BF16),
-            pltpu.VMEM((OWN, HALF), jnp.int32),
-            pltpu.VMEM((OWN, 1), F32),
-            pltpu.VMEM((1, HALF), F32),
-            pltpu.VMEM((2, OWN, HALF), F32),
-            pltpu.VMEM((OWN, LANES), F32),
-            pltpu.SemaphoreType.DMA((2 + 8 * CHUNKS,)),
-        ],
+        grid=(CHUNKS,),
+        in_specs=[half_spec] * 4
+        + [
+            pl.BlockSpec((TALL, HALF), lambda i: (i, half)),
+            pl.BlockSpec((TALL, 1), lambda i: (i, 0)),
+            pl.BlockSpec((1, HALF), lambda i: (0, half)),
+        ]
+        + ([whole(OWN), whole(HALF)] if half else []),
+        out_specs=(half_spec, half_spec, whole(OWN), whole(reach)),
+        scratch_shapes=[pltpu.VMEM((OWN, LANES), F32)],
         cost_estimate=pl.CostEstimate(
             flops=20 * OWN * HALF, bytes_accessed=5 << 20, transcendentals=0
         ),
-        compiler_params=GRANT,
+        compiler_params=SMALL,
     )(*parts, codes, rows, columns, *before)
 
 
 def first_kernel(half, gradient, second, codes, scale, *refs):
-    update, normed, peaks = refs[-3:]
+    update, normed, peaks, tops = refs[-4:]
     blocks = HALF // LANES
     for b in range(blocks):
         here = slice(b * LANES, (b + 1) * LANES)
@@ -302,13 +281,14 @@
         update[:, here] = new / CORR_ONE / (jnp.sqrt(second[:, here] / CORR_TWO) + 1e-08)
         peak = jnp.max(jnp.abs(new), axis=1, keepdims=True)
         normed[:, here] = (new / (peak + 1e-06)).astype(BF16)
-        peaks[:, block : block + 1] = peak
-    for b in range(blocks):
-        kept = (1 - half) * blocks + b
-        if half:
-            peaks[:, kept : kept + 1] = refs[0][:, kept : kept + 1]
-        else:
-            peaks[:, kept : kept + 1] = jnp.zeros((peaks.shape[0], 1), F32)
+        at = pl.ds(pl.multiple_of(pl.program_id(0) * TALL, TALL), TALL)
+        tops[at, b : b + 1] = peak
+
+    @pl.when(pl.program_id(0) == pl.num_programs(0) - 1)
+    def _():
+        mine = tops[...].T[:blocks]
+        rest = refs[0][:blocks, :] if half else mine
+        peaks[...] = jnp.concatenate([rest, mine] if half else [mine, rest], axis=0)
 
 
 def first_moment(half, gradient, second, codes, scale, before=()):
@@ -316,23 +296,25 @@
     blocks = scale.shape[1]
     half_spec = pl.BlockSpec((TALL, HALF), lambda i: (i, 0))
     there_spec = pl.BlockSpec((TALL, HALF), lambda i: (i, half))
-    peak_spec = pl.BlockSpec((TALL, blocks), lambda i: (i, 0))
+    scale_spec = pl.BlockSpec((TALL, blocks), lambda i: (i, 0))
+    peak_spec = pl.BlockSpec((blocks, rows), lambda i: (0, 0))
     return pl.pallas_call(
         functools.partial(first_kernel, half),
         out_shape=(
             jax.ShapeDtypeStruct((rows, width), F32),
             jax.ShapeDtypeStruct((rows, width), BF16),
-            jax.ShapeDtypeStruct((rows, blocks), F32),
+            jax.ShapeDtypeStruct((blocks, rows), F32),
         ),
         grid=(CHUNKS,),
-        in_specs=[half_spec, half_spec, there_spec, peak_spec]
+        in_specs=[half_spec, half_spec, there_spec, scale_spec]
         + ([peak_spec, ANY, ANY] if half else []),
         out_specs=(there_spec, there_spec, peak_spec),
+        scratch_shapes=[pltpu.VMEM((rows, LANES), F32)],
         input_output_aliases={5: 0, 6: 1} if half else {},
         cost_estimate=pl.CostEstimate(
             flops=40 * rows * HALF, bytes_accessed=5 << 20, transcendentals=rows * HALF
         ),
-        compiler_params=GRANT,
+        compiler_params=SMALL,
     )(gradient, second, codes, scale, *before)
 
 
@@ -351,7 +333,7 @@
     return pl.pallas_call(
         norm_kernel,
         out_shape=jax.ShapeDtypeStruct((OWN, 2 * HALF), BF16),
-        compiler_params=GRANT,
+        compiler_params=SMALL,
         name="norm",
     )(low, high, row_peak, column_peak)
 
@@ -386,7 +368,7 @@
     )
     both = ("dp", "row")
     partner = lax.ppermute(column_peak, "row", [(0, 1), (1, 0)])
-    for k in (1, 2):
+    for k in (1, 3):
         beside = lax.ppermute(row_peak, "col", [(z, z ^ k) for z in range(4)])
         row_peak = jnp.maximum(row_peak, beside)
     column_peak = ring_max(jnp.maximum(column_peak, partner), both, near)
@@ -398,7 +380,7 @@
     return (
         update_step,
         first_normed,
-        first_peak,
+        first_peak.T,
         second_normed,
         row_peak.reshape(-1),
         column_peak.reshape(-1),

time: 142 us -> 129 us (0.908)
  Pallas kernels: 62.7 us -> 50.9 us
  waiting for transfers between devices: 25.9 us -> 20 us
  local copies, waits for them, and re-layouts: 5.43 us -> 9.61 us
  starting transfers between devices: 34.7 us -> 36.2 us
    pallas_call x2, Pallas kernels: 8.41 us -> 1.77 us  [second_moment(): pl.pallas_call(functools.partial(second_kernel, half), out_shape=(jax.Sha...]
    ppermute x14, waiting for transfers between devices: 22.5 us -> 16.8 us  [send(): return lax.ppermute(value, ('dp', 'row'), pairs)]
    unnamed x24 -> x41, local copies, waits for them, and re-layouts: 4.49 us -> 9.38 us
    pallas_call x2, Pallas kernels: 8.81 us -> 5.44 us  [first_moment(): pl.pallas_call(functools.partial(first_kernel, half), out_shape=(jax.Shap...]
    add x0 -> x1, other arithmetic: none -> 1.8 us  [reduced(): own_low[3].astype(F32) + added_low_own.astype(F32)]
    pallas_call x1, Pallas kernels: 2.75 us -> 1.3 us  [norm_second(): pl.pallas_call(norm_kernel, out_shape=jax.ShapeDtypeStruct((OWN, 2 * HALF...]
  transfers between devices with their start and end apart: 23 -> 23, of which waited for: 9 -> 8; matrix products, arithmetic and copies ran while one was open for 9% -> 8% of each run, Pallas kernels for 33% -> 31%
where the time goes in v2:
time: 129 us
  Pallas kernels  50.9 us (39%)
  starting transfers between devices  36.2 us (28%)
  waiting for transfers between devices  20 us (16%)
  other arithmetic  11.1 us (9%)
  local copies, waits for them, and re-layouts  9.61 us (7%)
    pallas_call x4, Pallas kernels, product(): pl.pallas_call(functools.partial(product_kernel, base, bool(received)), o...  37.5 us
    ppermute x14, starting transfers between devices, send(): return lax.ppermute(value, ('dp', 'row'), pairs)  22.1 us
    ppermute x14, waiting for transfers between devices, send(): return lax.ppermute(value, ('dp', 'row'), pairs)  16.8 us
    unnamed x41, local copies, waits for them, and re-layouts  9.38 us
    convert_element_type x4, other arithmetic, add(): return (left.astype(F32) + right.astype(F32)).astype(BF16)  8.64 us
    ppermute x6, starting transfers between devices, ring_max(): parts.append(lax.ppermute(value, axis, way(k)))  8.03 us
    ppermute x2, starting transfers between devices, per_device(): beside = lax.ppermute(row_peak, 'col', [(z, z ^ k) for z in range(4)])  6.03 us
    pallas_call x2, Pallas kernels, first_moment(): pl.pallas_call(functools.partial(first_kernel, half), out_shape=(jax.Shap...  5.44 us
  transfers between devices with their start and end apart: 23, of which 8 were waited for; matrix products, arithmetic and copies ran while one was open for 8% of the time, Pallas kernels for 31%

profile of v2, /device:TPU:0, one launch (start us, length us, event | category | flops | bytes accessed | tf_op | source)
XLA Modules:
  0.0 128.9 jit_solution(14901792806098094644)
XLA Ops:
  0.7 0.1 stack.67
  0.8 0.6 pad_add_fusion.where
  1.4 9.0 %shard_map.121 = (bf16[4,448,512]{2,1,0:T(8,128)(2,1)}, bf16[4,448,512]{2,1,0:T(8,128)(2,1)}) custom-call(s32[32]{0:T(128)} %pad_add_fusion.where, bf16[1024,7168]{1,0:T(8,128)(2,1)} %hidden.7, bf16[1024,1024]{1,0:T(8,128)(2,1)} %upstream.7), custom_call_target="tpu_custom_call" | custom-call | flops 3758096384 | bytes 10485760 | tf_op jit(solution)/shard_map/pallas_call | solution.py:80
  10.4 1.7 %collective-permute-start.8 = (bf16[4,448,512]{2,1,0:T(8,128)(2,1)}, bf16[4,448,512]{2,1,0:T(8,128)(2,1)S(1)}, u32[]{:S(2)}, u32[]{:S(2)}) collective-permute-start(bf16[4,448,512]{2,1,0:T(8,128)(2,1)} %get-tuple-element.44), channel_id=1, source_target_pairs={{0,8},{4,36},{8,16},{12,44},{16,24},{20,52},{24,0},{28,60},{32,40}... | collective-permute-start | bytes 5505032 | tf_op jit(solution)/shard_map/ppermute | solution.py:124
  12.1 1.6 %collective-permute-start.2 = (bf16[4,448,512]{2,1,0:T(8,128)(2,1)}, bf16[4,448,512]{2,1,0:T(8,128)(2,1)}, u32[]{:S(2)}, u32[]{:S(2)}) collective-permute-start(bf16[4,448,512]{2,1,0:T(8,128)(2,1)} %get-tuple-element.38), channel_id=1, source_target_pairs={{0,24},{4,100},{8,0},{12,108},{16,8},{20,116},{24,16},{28,124},{32... | collective-permute-start | bytes 5505032 | tf_op jit(solution)/shard_map/ppermute | solution.py:124
  13.8 9.0 %shard_map.119 = (bf16[4,448,512]{2,1,0:T(8,128)(2,1)}, bf16[4,448,512]{2,1,0:T(8,128)(2,1)}) custom-call(s32[32]{0:T(128)} %pad_add_fusion.where, bf16[1024,7168]{1,0:T(8,128)(2,1)} %hidden.7, bf16[1024,1024]{1,0:T(8,128)(2,1)} %upstream.7), custom_call_target="tpu_custom_call" | custom-call | flops 3758096384 | bytes 10485760 | tf_op jit(solution)/shard_map/pallas_call | solution.py:80
  22.8 0.7 collective-permute-start.1
  23.4 9.1 %shard_map.118 = (bf16[4,448,512]{2,1,0:T(8,128)(2,1)}, bf16[4,448,512]{2,1,0:T(8,128)(2,1)}) custom-call(s32[32]{0:T(128)} %pad_add_fusion.where, bf16[1024,7168]{1,0:T(8,128)(2,1)} %hidden.7, bf16[1024,1024]{1,0:T(8,128)(2,1)} %upstream.7), custom_call_target="tpu_custom_call" | custom-call | flops 3758096384 | bytes 10485760 | tf_op jit(solution)/shard_map/pallas_call | solution.py:80
  32.5 2.9 %collective-permute-start = (bf16[4,448,512]{2,1,0:T(8,128)(2,1)}, bf16[4,448,512]{2,1,0:T(8,128)(2,1)}, u32[]{:S(2)}, u32[]{:S(2)}) collective-permute-start(bf16[4,448,512]{2,1,0:T(8,128)(2,1)} %get-tuple-element.34), channel_id=1, source_target_pairs={{0,24},{4,100},{8,0},{12,108},{16,8},{20,116},{24,16},{28,124},{32... | collective-permute-start | bytes 5505032 | tf_op jit(solution)/shard_map/ppermute | solution.py:124
  35.4 1.2 copy-done.16
  36.6 1.9 %add_convert_fusion = bf16[3,448,512]{2,1,0:T(8,128)(2,1)S(1)} fusion(bf16[4,448,512]{2,1,0:T(8,128)(2,1)S(1)} %collective-permute-done.8, bf16[4,448,512]{2,1,0:T(8,128)(2,1)} %get-tuple-element.43), kind=kLoop, calls=%fused_computation | loop fusion | flops 2752512 | bytes 4128768 | tf_op jit(solution)/shard_map/convert_element_type | solution.py:172
  38.5 0.2 collective-permute-start.10
  38.7 2.8 %add_convert_fusion.1 = bf16[3,448,512]{2,1,0:T(8,128)(2,1)} fusion(bf16[4,448,512]{2,1,0:T(8,128)(2,1)} %collective-permute-done.2, bf16[4,448,512]{2,1,0:T(8,128)(2,1)S(1)} %copy-done.17), kind=kLoop, calls=%fused_computation.1 | loop fusion | flops 2752512 | bytes 4128768 | tf_op jit(solution)/shard_map/convert_element_type | solution.py:172
  41.6 3.1 %collective-permute-start.4 = (bf16[3,448,512]{2,1,0:T(8,128)(2,1)}, bf16[3,448,512]{2,1,0:T(8,128)(2,1)S(1)}, u32[]{:S(2)}, u32[]{:S(2)}) collective-permute-start(bf16[3,448,512]{2,1,0:T(8,128)(2,1)} %add_convert_fusion.1), channel_id=1, source_target_pairs={{0,24},{4,100},{8,0},{12,108},{16,8},{20,116},{24,16},{28,124},{32... | collective-permute-start | bytes 4128776 | tf_op jit(solution)/shard_map/ppermute | solution.py:124
  44.6 2.0 %fusion.1 = bf16[448,512]{1,0:T(8,128)(2,1)} fusion(bf16[4,448,512]{2,1,0:T(8,128)(2,1)} %copy-done.16, bf16[4,448,512]{2,1,0:T(8,128)(2,1)} %get-tuple-element.43), kind=kLoop, calls=%fused_computation.7 | loop fusion | flops 917504 | bytes 1376256 | tf_op jit(solution)/shard_map/convert_element_type | solution.py:172
  46.7 1.9 %fusion = bf16[448,512]{1,0:T(8,128)(2,1)} fusion(bf16[4,448,512]{2,1,0:T(8,128)(2,1)} %collective-permute-done.2, bf16[4,448,512]{2,1,0:T(8,128)(2,1)S(1)} %copy-done.17), kind=kLoop, calls=%fused_computation.6 | loop fusion | flops 917504 | bytes 1376256 | tf_op jit(solution)/shard_map/convert_element_type | solution.py:172
  48.6 6.3 %collective-permute-done.1.refs_1_ = bf16[4,448,512]{2,1,0:T(8,128)(2,1)S(1)} collective-permute-done((bf16[4,448,512]{2,1,0:T(8,128)(2,1)}, bf16[4,448,512]{2,1,0:T(8,128)(2,1)S(1)}, u32[]{:S(2)}, u32[]{:S(2)}) %collective-permute-start.1) | collective-permute-done | bytes 1835040 | tf_op jit(solution)/shard_map/ppermute | solution.py:124
  54.8 1.7 %collective-permute-start.3 = (bf16[448,512]{1,0:T(8,128)(2,1)}, bf16[448,512]{1,0:T(8,128)(2,1)}, u32[]{:S(2)}, u32[]{:S(2)}) collective-permute-start(bf16[448,512]{1,0:T(8,128)(2,1)} %fusion), channel_id=1, source_target_pairs={{0,24},{4,100},{8,0},{12,108},{16,8},{20,116},{24,16},{28,124},{32... | collective-permute-start | bytes 1376264 | tf_op jit(solution)/shard_map/ppermute | solution.py:124
  56.5 10.4 %shard_map.120 = (bf16[4,448,512]{2,1,0:T(8,128)(2,1)}, bf16[4,448,512]{2,1,0:T(8,128)(2,1)}) custom-call(s32[32]{0:T(128)} %pad_add_fusion.where, bf16[1024,7168]{1,0:T(8,128)(2,1)} %hidden.7, bf16[1024,1024]{1,0:T(8,128)(2,1)} %upstream.7, bf16[4,448,512]{2,1,0:T(8,128)(2,1)} %collective-permute-done.refs_0_, bf16[4,448,512]{2,1,0:T(8,128)(2,1)} %copy-done.15), custom_call_target="tpu_custom_call" | custom-call | flops 3758096384 | bytes 10485760 | tf_op jit(solution)/shard_map/pallas_call | solution.py:80
  66.9 2.6 %collective-permute-done.10.got = bf16[3,448,512]{2,1,0:T(8,128)(2,1)S(1)} collective-permute-done((bf16[3,448,512]{2,1,0:T(8,128)(2,1)S(1)}, bf16[3,448,512]{2,1,0:T(8,128)(2,1)S(1)}, u32[]{:S(2)}, u32[]{:S(2)}) %collective-permute-start.10) | collective-permute-done | bytes 1376288 | tf_op jit(solution)/shard_map/ppermute | solution.py:124
  69.6 2.3 %shard_map.123 = (bf16[448,512]{1,0:T(8,128)(2,1)S(1)}, bf16[448,512]{1,0:T(8,128)(2,1)}, bf16[448,512]{1,0:T(8,128)(2,1)S(1)}) custom-call(bf16[4,448,512]{2,1,0:T(8,128)(2,1)} %get-tuple-element.42.kept, bf16[3,448,512]{2,1,0:T(8,128)(2,1)S(1)} %collective-permute-done.10.got), custom_call_target="tpu_custom_call" | custom-call | flops 688128 | bytes 4194304 | tf_op jit(solution)/shard_map/pallas_call | solution.py:153
  71.9 0.0 copy-start.19
  71.9 3.4 %collective-permute-start.11 = (bf16[448,512]{1,0:T(8,128)(2,1)S(1)}, bf16[448,512]{1,0:T(8,128)(2,1)S(1)}, u32[]{:S(2)}, u32[]{:S(2)}) collective-permute-start(bf16[448,512]{1,0:T(8,128)(2,1)S(1)} %get-tuple-element.45), channel_id=1, source_target_pairs={{0,64},{4,20},{8,72},{12,28},{16,80},{20,4},{24,88},{28,12},{32,96... | collective-permute-start | bytes 1376264 | tf_op jit(solution)/shard_map/ppermute | solution.py:124
  75.3 0.7 collective-permute-start.12
  76.0 2.6 %collective-permute-start.13 = (bf16[448,512]{1,0:T(8,128)(2,1)S(1)}, bf16[448,512]{1,0:T(8,128)(2,1)S(1)}, u32[]{:S(2)}, u32[]{:S(2)}) collective-permute-start(bf16[448,512]{1,0:T(8,128)(2,1)S(1)} %get-tuple-element.47), channel_id=1, source_target_pairs={{0,96},{4,28},{8,104},{12,4},{16,112},{20,12},{24,120},{28,20},{32... | collective-permute-start | bytes 1376264 | tf_op jit(solution)/shard_map/ppermute | solution.py:124
  78.6 2.6 %shard_map.122 = (bf16[448,512]{1,0:T(8,128)(2,1)}, bf16[448,512]{1,0:T(8,128)(2,1)}, bf16[448,512]{1,0:T(8,128)(2,1)}) custom-call(bf16[4,448,512]{2,1,0:T(8,128)(2,1)} %get-tuple-element.36.kept, bf16[3,448,512]{2,1,0:T(8,128)(2,1)S(1)} %collective-permute-done.4.got), custom_call_target="tpu_custom_call" | custom-call | flops 688128 | bytes 4194304 | tf_op jit(solution)/shard_map/pallas_call | solution.py:153
  81.2 0.1 collective-permute-start.5
  81.3 1.0 collective-permute-done.3
  82.3 2.1 %collective-permute-start.6 = (bf16[448,512]{1,0:T(8,128)(2,1)}, bf16[448,512]{1,0:T(8,128)(2,1)S(1)}, u32[]{:S(2)}, u32[]{:S(2)}) collective-permute-start(bf16[448,512]{1,0:T(8,128)(2,1)} %get-tuple-element.40), channel_id=1, source_target_pairs={{0,32},{4,12},{8,40},{12,20},{16,48},{20,28},{24,56},{28,4},{32,64... | collective-permute-start | bytes 1376264 | tf_op jit(solution)/shard_map/ppermute | solution.py:124
  84.4 1.4 %collective-permute-start.7 = (bf16[448,512]{1,0:T(8,128)(2,1)}, bf16[448,512]{1,0:T(8,128)(2,1)S(1)}, u32[]{:S(2)}, u32[]{:S(2)}) collective-permute-start(bf16[448,512]{1,0:T(8,128)(2,1)} %get-tuple-element.41), channel_id=1, source_target_pairs={{0,96},{4,28},{8,104},{12,4},{16,112},{20,12},{24,120},{28,20},{32... | collective-permute-start | bytes 1376264 | tf_op jit(solution)/shard_map/ppermute | solution.py:124
  85.8 0.1 copy.18.rows
  86.0 0.0 copy-start
  86.0 0.0 copy-start.13
  86.0 1.8 %convert_add_fusion = (f32[448,512]{1,0:T(8,128)S(1)}, f32[448,512]{1,0:T(8,128)S(1)}) fusion(bf16[448,512]{1,0:T(8,128)(2,1)} %collective-permute-done.9, bf16[4,448,512]{2,1,0:T(8,128)(2,1)} %get-tuple-element.42.kept, bf16[448,512]{1,0:T(8,128)(2,1)} %collective-permute-done.3, bf16[4,448,512]{2,1,0:T(8,128)(2,1)} %get-tuple-element.36.kept), kind=kLoop, calls=%fused_computation.2 | loop fusion | flops 1376256 | bytes 3670016 | tf_op jit(solution)/shard_map/add | solution.py:192
  87.8 0.2 copy-done
  88.1 0.9 shard_map.124
  89.0 0.9 copy-done.6
  89.9 2.1 %collective-permute-done.5.far = bf16[448,512]{1,0:T(8,128)(2,1)S(1)} collective-permute-done((bf16[448,512]{1,0:T(8,128)(2,1)}, bf16[448,512]{1,0:T(8,128)(2,1)S(1)}, u32[]{:S(2)}, u32[]{:S(2)}) %collective-permute-start.5) | collective-permute-done | bytes 458784 | tf_op jit(solution)/shard_map/ppermute | solution.py:124
  92.0 4.8 %collective-permute-done.6.up = bf16[448,512]{1,0:T(8,128)(2,1)S(1)} collective-permute-done((bf16[448,512]{1,0:T(8,128)(2,1)}, bf16[448,512]{1,0:T(8,128)(2,1)S(1)}, u32[]{:S(2)}, u32[]{:S(2)}) %collective-permute-start.6) | collective-permute-done | bytes 458784 | tf_op jit(solution)/shard_map/ppermute | solution.py:124
  96.8 0.8 copy-done.8
  97.5 0.8 copy-done.10
  98.3 1.0 copy-done.9
  99.3 1.0 copy-done.11
  100.4 0.9 shard_map.125
  101.3 0.0 copy-start.4
  101.3 0.9 copy-done.4
  102.2 1.2 collective-permute-done.16
  103.4 1.7 %collective-permute-start.19 = (f32[1,1024]{1,0:T(1,128)S(1)}, f32[1,1024]{1,0:T(1,128)S(1)}, u32[]{:S(2)}, u32[]{:S(2)}) collective-permute-start(f32[1,1024]{1,0:T(1,128)S(1)} %max.29), channel_id=1, source_target_pairs={{0,24},{4,100},{8,0},{12,108},{16,8},{20,116},{24,16},{28,124},{32... | collective-permute-start | bytes 12296 | tf_op jit(solution)/shard_map/ppermute | solution.py:344
  105.1 0.8 collective-permute-start.18
  105.8 0.9 collective-permute-start.17
  106.7 1.9 %collective-permute-start.14 = (f32[1,448]{1,0:T(1,128)S(1)}, f32[1,448]{1,0:T(1,128)S(1)}, u32[]{:S(2)}, u32[]{:S(2)}) collective-permute-start(f32[1,448]{1,0:T(1,128)S(1)} %get-tuple-element.60), channel_id=1, source_target_pairs={{0,1},{1,0},{2,3},{3,2},{4,5},{5,4},{6,7},{7,6},{8,9},{9,8},{10,11... | collective-permute-start | bytes 5384 | tf_op jit(solution)/shard_map/ppermute | solution.py:372
  108.6 1.5 %collective-permute-done.18 = f32[1,1024]{1,0:T(1,128)S(1)} collective-permute-done((f32[1,1024]{1,0:T(1,128)S(1)}, f32[1,1024]{1,0:T(1,128)S(1)}, u32[]{:S(2)}, u32[]{:S(2)}) %collective-permute-start.18) | collective-permute-done | bytes 4128 | tf_op jit(solution)/shard_map/ppermute | solution.py:344
  110.2 0.5 collective-permute-done.17
  110.7 2.3 %collective-permute-start.22 = (f32[1,1024]{1,0:T(1,128)S(1)}, f32[1,1024]{1,0:T(1,128)S(1)}, u32[]{:S(2)}, u32[]{:S(2)}) collective-permute-start(f32[1,1024]{1,0:T(1,128)S(1)} %maximum_maximum_fusion.1), channel_id=1, source_target_pairs={{0,96},{4,28},{8,104},{12,4},{16,112},{20,12},{24,120},{28,20},{32... | collective-permute-start | bytes 12296 | tf_op jit(solution)/shard_map/ppermute | solution.py:344
  113.0 1.5 %collective-permute-start.21 = (f32[1,1024]{1,0:T(1,128)S(1)}, f32[1,1024]{1,0:T(1,128)S(1)}, u32[]{:S(2)}, u32[]{:S(2)}) collective-permute-start(f32[1,1024]{1,0:T(1,128)S(1)} %maximum_maximum_fusion.1), channel_id=1, source_target_pairs={{0,64},{4,20},{8,72},{12,28},{16,80},{20,4},{24,88},{28,12},{32,96... | collective-permute-start | bytes 12296 | tf_op jit(solution)/shard_map/ppermute | solution.py:344
  114.6 0.8 collective-permute-start.20
  115.4 0.1 copy.20.scale
  115.5 4.1 %collective-permute-start.15 = (f32[1,448]{1,0:T(1,128)S(1)}, f32[1,448]{1,0:T(1,128)S(1)}, u32[]{:S(2)}, u32[]{:S(2)}) collective-permute-start(f32[1,448]{1,0:T(1,128)S(1)} %max.27), channel_id=1, source_target_pairs={{0,3},{1,2},{2,1},{3,0},{4,7},{5,6},{6,5},{7,4},{8,11},{9,10},{10,... | collective-permute-start | bytes 5384 | tf_op jit(solution)/shard_map/ppermute | solution.py:372
  119.7 1.2 copy-done.3
  120.8 1.2 copy-done.7
  122.0 2.7 %shard_map.126 = (f32[448,1024]{1,0:T(8,128)}, bf16[448,1024]{1,0:T(8,128)(2,1)}, f32[8,448]{1,0:T(8,128)S(1)}) custom-call(f32[448,512]{1,0:T(8,128)S(1)} %copy-done.7, f32[448,512]{1,0:T(8,128)S(1)} %copy-done.3, s32[448,1024]{1,0:T(8,128)S(1)} %copy-done.1, f32[448,8]{1,0:T(8,128)S(1)} %copy.20.scale), custom_call_target="tpu_custom_call" | custom-call | flops 9175040 | bytes 5242880 | tf_op jit(solution)/shard_map/pallas_call | solution.py:301
  124.7 2.7 %shard_map.127 = (f32[448,1024]{1,0:T(8,128)}, bf16[448,1024]{1,0:T(8,128)(2,1)}, f32[8,448]{1,0:T(8,128)}) custom-call(f32[448,512]{1,0:T(8,128)S(1)} %copy-done.5, f32[448,512]{1,0:T(8,128)S(1)} %get-tuple-element.51.second.high, s32[448,1024]{1,0:T(8,128)S(1)} %copy-done.1, ...), custom_call_target="tpu_custom_call", output_to_operand_aliasing={{0}: (5, {}), {1}: (6, {})} | custom-call | flops 9175040 | bytes 5242880 | tf_op jit(solution)/shard_map/pallas_call | solution.py:301
  127.5 0.0 copy-start.12
  127.6 1.3 %norm.1 = bf16[448,1024]{1,0:T(8,128)(2,1)} custom-call(f32[448,512]{1,0:T(8,128)S(1)} %copy-done.3, f32[448,512]{1,0:T(8,128)S(1)} %get-tuple-element.51.second.high, f32[1,448]{1,0:T(1,128)S(1)} %max.28.row_peak, f32[1,1024]{1,0:T(1,128)S(1)} %maximum_maximum_fusion.column_peak), custom_call_target="tpu_custom_call" | custom-call | tf_op jit(solution)/shard_map/norm/pallas_call | solution.py:333
  (48 shorter events, 0.1 us)
Async XLA Ops:
  10.4 24.9 %collective-permute-start.8 = (bf16[4,448,512]{2,1,0:T(8,128)(2,1)}, bf16[4,448,512]{2,1,0:T(8,128)(2,1)S(1)}, u32[]{:S(2)}, u32[]{:S(2)}) collective-permute-start(bf16[4,448,512]{2,1,0:T(8,128)(2,1)} %get-tuple-element.44), channel_id=1, source_target_pairs={{0,8},{4,36},{8,16},{12,44},{16,24},{20,52},{24,0},{28,60},{32,40}... | collective-permute-start | bytes 5505032 | tf_op jit(solution)/shard_map/ppermute | solution.py:124
  12.1 26.6 %collective-permute-start.2 = (bf16[4,448,512]{2,1,0:T(8,128)(2,1)}, bf16[4,448,512]{2,1,0:T(8,128)(2,1)}, u32[]{:S(2)}, u32[]{:S(2)}) collective-permute-start(bf16[4,448,512]{2,1,0:T(8,128)(2,1)} %get-tuple-element.38), channel_id=1, source_target_pairs={{0,24},{4,100},{8,0},{12,108},{16,8},{20,116},{24,16},{28,124},{32... | collective-permute-start | bytes 5505032 | tf_op jit(solution)/shard_map/ppermute | solution.py:124
  22.8 32.1 %collective-permute-start.1 = (bf16[4,448,512]{2,1,0:T(8,128)(2,1)}, bf16[4,448,512]{2,1,0:T(8,128)(2,1)S(1)}, u32[]{:S(2)}, u32[]{:S(2)}) collective-permute-start(bf16[4,448,512]{2,1,0:T(8,128)(2,1)} %get-tuple-element.35), channel_id=1, source_target_pairs={{0,8},{4,36},{8,16},{12,44},{16,24},{20,52},{24,0},{28,60},{32,40}... | collective-permute-start | bytes 5505032 | tf_op jit(solution)/shard_map/ppermute | solution.py:124
  32.5 24.0 %collective-permute-start = (bf16[4,448,512]{2,1,0:T(8,128)(2,1)}, bf16[4,448,512]{2,1,0:T(8,128)(2,1)}, u32[]{:S(2)}, u32[]{:S(2)}) collective-permute-start(bf16[4,448,512]{2,1,0:T(8,128)(2,1)} %get-tuple-element.34), channel_id=1, source_target_pairs={{0,24},{4,100},{8,0},{12,108},{16,8},{20,116},{24,16},{28,124},{32... | collective-permute-start | bytes 5505032 | tf_op jit(solution)/shard_map/ppermute | solution.py:124
  35.4 1.2 copy-start.16
  36.6 2.1 %copy-start.17 = (bf16[4,448,512]{2,1,0:T(8,128)(2,1)S(1)}, bf16[4,448,512]{2,1,0:T(8,128)(2,1)}, u32[]{:S(2)}) copy-start(bf16[4,448,512]{2,1,0:T(8,128)(2,1)} %get-tuple-element.37) | copy-start | bytes 5505028
  38.5 31.1 %collective-permute-start.10 = (bf16[3,448,512]{2,1,0:T(8,128)(2,1)S(1)}, bf16[3,448,512]{2,1,0:T(8,128)(2,1)S(1)}, u32[]{:S(2)}, u32[]{:S(2)}) collective-permute-start(bf16[3,448,512]{2,1,0:T(8,128)(2,1)S(1)} %add_convert_fusion), channel_id=1, source_target_pairs={{0,8},{4,36},{8,16},{12,44},{16,24},{20,52},{24,0},{28,60},{32,40}... | collective-permute-start | bytes 4128776 | tf_op jit(solution)/shard_map/ppermute | solution.py:124
  41.6 34.4 %collective-permute-start.4 = (bf16[3,448,512]{2,1,0:T(8,128)(2,1)}, bf16[3,448,512]{2,1,0:T(8,128)(2,1)S(1)}, u32[]{:S(2)}, u32[]{:S(2)}) collective-permute-start(bf16[3,448,512]{2,1,0:T(8,128)(2,1)} %add_convert_fusion.1), channel_id=1, source_target_pairs={{0,24},{4,100},{8,0},{12,108},{16,8},{20,116},{24,16},{28,124},{32... | collective-permute-start | bytes 4128776 | tf_op jit(solution)/shard_map/ppermute | solution.py:124
  46.7 34.5 %collective-permute-start.9 = (bf16[448,512]{1,0:T(8,128)(2,1)}, bf16[448,512]{1,0:T(8,128)(2,1)}, u32[]{:S(2)}, u32[]{:S(2)}) collective-permute-start(bf16[448,512]{1,0:T(8,128)(2,1)} %fusion.1), channel_id=1, source_target_pairs={{0,8},{4,36},{8,16},{12,44},{16,24},{20,52},{24,0},{28,60},{32,40}... | collective-permute-start | bytes 1376264 | tf_op jit(solution)/shard_map/ppermute | solution.py:124
  54.8 1.7 %copy-start.15 = (bf16[4,448,512]{2,1,0:T(8,128)(2,1)}, bf16[4,448,512]{2,1,0:T(8,128)(2,1)S(1)}, u32[]{:S(2)}) copy-start(bf16[4,448,512]{2,1,0:T(8,128)(2,1)S(1)} %collective-permute-done.1.refs_1_) | copy-start | bytes 5505028
  54.8 27.5 %collective-permute-start.3 = (bf16[448,512]{1,0:T(8,128)(2,1)}, bf16[448,512]{1,0:T(8,128)(2,1)}, u32[]{:S(2)}, u32[]{:S(2)}) collective-permute-start(bf16[448,512]{1,0:T(8,128)(2,1)} %fusion), channel_id=1, source_target_pairs={{0,24},{4,100},{8,0},{12,108},{16,8},{20,116},{24,16},{28,124},{32... | collective-permute-start | bytes 1376264 | tf_op jit(solution)/shard_map/ppermute | solution.py:124
  71.9 13.9 %copy-start.19 = (f32[448]{0:T(512)S(1)}, f32[448]{0:T(512)}, u32[]{:S(2)}) copy-start(f32[448]{0:T(512)} %param.12) | copy-start | bytes 5380
  71.9 12.5 %collective-permute-start.11 = (bf16[448,512]{1,0:T(8,128)(2,1)S(1)}, bf16[448,512]{1,0:T(8,128)(2,1)S(1)}, u32[]{:S(2)}, u32[]{:S(2)}) collective-permute-start(bf16[448,512]{1,0:T(8,128)(2,1)S(1)} %get-tuple-element.45), channel_id=1, source_target_pairs={{0,64},{4,20},{8,72},{12,28},{16,80},{20,4},{24,88},{28,12},{32,96... | collective-permute-start | bytes 1376264 | tf_op jit(solution)/shard_map/ppermute | solution.py:124
  75.3 12.5 %collective-permute-start.12 = (bf16[448,512]{1,0:T(8,128)(2,1)}, bf16[448,512]{1,0:T(8,128)(2,1)S(1)}, u32[]{:S(2)}, u32[]{:S(2)}) collective-permute-start(bf16[448,512]{1,0:T(8,128)(2,1)} %get-tuple-element.46), channel_id=1, source_target_pairs={{0,32},{4,12},{8,40},{12,20},{16,48},{20,28},{24,56},{28,4},{32,64... | collective-permute-start | bytes 1376264 | tf_op jit(solution)/shard_map/ppermute | solution.py:124
  76.0 11.8 %collective-permute-start.13 = (bf16[448,512]{1,0:T(8,128)(2,1)S(1)}, bf16[448,512]{1,0:T(8,128)(2,1)S(1)}, u32[]{:S(2)}, u32[]{:S(2)}) collective-permute-start(bf16[448,512]{1,0:T(8,128)(2,1)S(1)} %get-tuple-element.47), channel_id=1, source_target_pairs={{0,96},{4,28},{8,104},{12,4},{16,112},{20,12},{24,120},{28,20},{32... | collective-permute-start | bytes 1376264 | tf_op jit(solution)/shard_map/ppermute | solution.py:124
  81.2 10.8 %collective-permute-start.5 = (bf16[448,512]{1,0:T(8,128)(2,1)}, bf16[448,512]{1,0:T(8,128)(2,1)S(1)}, u32[]{:S(2)}, u32[]{:S(2)}) collective-permute-start(bf16[448,512]{1,0:T(8,128)(2,1)} %get-tuple-element.39), channel_id=1, source_target_pairs={{0,64},{4,20},{8,72},{12,28},{16,80},{20,4},{24,88},{28,12},{32,96... | collective-permute-start | bytes 1376264 | tf_op jit(solution)/shard_map/ppermute | solution.py:124
  82.3 14.5 %collective-permute-start.6 = (bf16[448,512]{1,0:T(8,128)(2,1)}, bf16[448,512]{1,0:T(8,128)(2,1)S(1)}, u32[]{:S(2)}, u32[]{:S(2)}) collective-permute-start(bf16[448,512]{1,0:T(8,128)(2,1)} %get-tuple-element.40), channel_id=1, source_target_pairs={{0,32},{4,12},{8,40},{12,20},{16,48},{20,28},{24,56},{28,4},{32,64... | collective-permute-start | bytes 1376264 | tf_op jit(solution)/shard_map/ppermute | solution.py:124
  84.4 13.1 %collective-permute-start.7 = (bf16[448,512]{1,0:T(8,128)(2,1)}, bf16[448,512]{1,0:T(8,128)(2,1)S(1)}, u32[]{:S(2)}, u32[]{:S(2)}) collective-permute-start(bf16[448,512]{1,0:T(8,128)(2,1)} %get-tuple-element.41), channel_id=1, source_target_pairs={{0,96},{4,28},{8,104},{12,4},{16,112},{20,12},{24,120},{28,20},{32... | collective-permute-start | bytes 1376264 | tf_op jit(solution)/shard_map/ppermute | solution.py:124
  86.0 2.1 %copy-start = (s32[448,1024]{1,0:T(8,128)S(1)}, s32[448,1024]{1,0:T(8,128)}, u32[]{:S(2)}) copy-start(s32[448,1024]{1,0:T(8,128)} %codes.5) | copy-start | bytes 5505028
  86.0 2.0 %copy-start.13 = (f32[1024]{0:T(1024)S(1)}, f32[1024]{0:T(1024)}, u32[]{:S(2)}) copy-start(f32[1024]{0:T(1024)} %param.13) | copy-start | bytes 12292
  88.9 0.9 copy-start.6
  89.9 11.4 %copy-start.2 = (f32[448,512]{1,0:T(8,128)}, f32[448,512]{1,0:T(8,128)S(1)}, u32[]{:S(2)}) copy-start(f32[448,512]{1,0:T(8,128)S(1)} %get-tuple-element.53.second.low) | copy-start | bytes 2752516
  96.8 0.8 copy-start.8
  97.5 0.8 copy-start.10
  98.3 1.0 copy-start.9
  99.3 1.0 copy-start.11
  100.4 15.0 %copy-start.18 = (f32[448,8]{0,1:T(8,128)S(1)}, f32[448,8]{0,1:T(8,128)}, u32[]{:S(2)}) copy-start(f32[448,8]{0,1:T(8,128)} %param.10) | copy-start | bytes 43012
  100.4 19.3 %copy-start.1 = (s32[448,1024]{1,0:T(8,128)S(1)}, s32[448,1024]{1,0:T(8,128)}, u32[]{:S(2)}) copy-start(s32[448,1024]{1,0:T(8,128)} %codes.7) | copy-start | bytes 5505028
  101.3 0.9 copy-start.4
  102.2 1.2 collective-permute-start.16
  103.4 5.2 %collective-permute-start.19 = (f32[1,1024]{1,0:T(1,128)S(1)}, f32[1,1024]{1,0:T(1,128)S(1)}, u32[]{:S(2)}, u32[]{:S(2)}) collective-permute-start(f32[1,1024]{1,0:T(1,128)S(1)} %max.29), channel_id=1, source_target_pairs={{0,24},{4,100},{8,0},{12,108},{16,8},{20,116},{24,16},{28,124},{32... | collective-permute-start | bytes 12296 | tf_op jit(solution)/shard_map/ppermute | solution.py:344
  105.1 5.1 %collective-permute-start.18 = (f32[1,1024]{1,0:T(1,128)S(1)}, f32[1,1024]{1,0:T(1,128)S(1)}, u32[]{:S(2)}, u32[]{:S(2)}) collective-permute-start(f32[1,1024]{1,0:T(1,128)S(1)} %max.29), channel_id=1, source_target_pairs={{0,16},{4,68},{8,24},{12,76},{16,0},{20,84},{24,8},{28,92},{32,48}... | collective-permute-start | bytes 12296 | tf_op jit(solution)/shard_map/ppermute | solution.py:344
  105.8 4.8 %collective-permute-start.17 = (f32[1,1024]{1,0:T(1,128)S(1)}, f32[1,1024]{1,0:T(1,128)S(1)}, u32[]{:S(2)}, u32[]{:S(2)}) collective-permute-start(f32[1,1024]{1,0:T(1,128)S(1)} %max.29), channel_id=1, source_target_pairs={{0,8},{4,36},{8,16},{12,44},{16,24},{20,52},{24,0},{28,60},{32,40}... | collective-permute-start | bytes 12296 | tf_op jit(solution)/shard_map/ppermute | solution.py:344
  106.7 8.8 %collective-permute-start.14 = (f32[1,448]{1,0:T(1,128)S(1)}, f32[1,448]{1,0:T(1,128)S(1)}, u32[]{:S(2)}, u32[]{:S(2)}) collective-permute-start(f32[1,448]{1,0:T(1,128)S(1)} %get-tuple-element.60), channel_id=1, source_target_pairs={{0,1},{1,0},{2,3},{3,2},{4,5},{5,4},{6,7},{7,6},{8,9},{9,8},{10,11... | collective-permute-start | bytes 5384 | tf_op jit(solution)/shard_map/ppermute | solution.py:372
  110.7 16.8 %collective-permute-start.22 = (f32[1,1024]{1,0:T(1,128)S(1)}, f32[1,1024]{1,0:T(1,128)S(1)}, u32[]{:S(2)}, u32[]{:S(2)}) collective-permute-start(f32[1,1024]{1,0:T(1,128)S(1)} %maximum_maximum_fusion.1), channel_id=1, source_target_pairs={{0,96},{4,28},{8,104},{12,4},{16,112},{20,12},{24,120},{28,20},{32... | collective-permute-start | bytes 12296 | tf_op jit(solution)/shard_map/ppermute | solution.py:344
  113.0 14.5 %collective-permute-start.21 = (f32[1,1024]{1,0:T(1,128)S(1)}, f32[1,1024]{1,0:T(1,128)S(1)}, u32[]{:S(2)}, u32[]{:S(2)}) collective-permute-start(f32[1,1024]{1,0:T(1,128)S(1)} %maximum_maximum_fusion.1), channel_id=1, source_target_pairs={{0,64},{4,20},{8,72},{12,28},{16,80},{20,4},{24,88},{28,12},{32,96... | collective-permute-start | bytes 12296 | tf_op jit(solution)/shard_map/ppermute | solution.py:344
  114.6 13.0 %collective-permute-start.20 = (f32[1,1024]{1,0:T(1,128)S(1)}, f32[1,1024]{1,0:T(1,128)S(1)}, u32[]{:S(2)}, u32[]{:S(2)}) collective-permute-start(f32[1,1024]{1,0:T(1,128)S(1)} %maximum_maximum_fusion.1), channel_id=1, source_target_pairs={{0,32},{4,12},{8,40},{12,20},{16,48},{20,28},{24,56},{28,4},{32,64... | collective-permute-start | bytes 12296 | tf_op jit(solution)/shard_map/ppermute | solution.py:344
  115.5 11.9 %collective-permute-start.15 = (f32[1,448]{1,0:T(1,128)S(1)}, f32[1,448]{1,0:T(1,128)S(1)}, u32[]{:S(2)}, u32[]{:S(2)}) collective-permute-start(f32[1,448]{1,0:T(1,128)S(1)} %max.27), channel_id=1, source_target_pairs={{0,3},{1,2},{2,1},{3,0},{4,7},{5,6},{6,5},{7,4},{8,11},{9,10},{10,... | collective-permute-start | bytes 5384 | tf_op jit(solution)/shard_map/ppermute | solution.py:372
  119.7 1.2 copy-start.3
  120.8 1.2 copy-start.7
  122.0 2.7 %copy-start.5 = (f32[448,512]{1,0:T(8,128)S(1)}, f32[448,512]{1,0:T(8,128)}, u32[]{:S(2)}) copy-start(f32[448,512]{1,0:T(8,128)} %copy-done.4) | copy-start | bytes 2752516
  127.5 1.4 %copy-start.14 = (f32[1,448]{1,0:T(1,128)}, f32[1,448]{1,0:T(1,128)S(1)}, u32[]{:S(2)}) copy-start(f32[1,448]{1,0:T(1,128)S(1)} %max.28.row_peak) | copy-start | bytes 5380
  127.5 1.3 %copy-start.12 = (f32[1,1024]{1,0:T(1,128)}, f32[1,1024]{1,0:T(1,128)S(1)}, u32[]{:S(2)}) copy-start(f32[1,1024]{1,0:T(1,128)S(1)} %maximum_maximum_fusion.column_peak) | copy-start | bytes 12292

commit v3 on v2

--- a/solution.py
+++ b/solution.py
@@ -32,21 +32,33 @@
     return lax.dot_general(left, right, (((0,), (0,)), ((), ())), preferred_element_type=F32)
 
 
-def product_kernel(base, added, where, hidden, upstream, *refs):
-    received = refs[:2] if added else ()
-    outs = refs[len(received) : len(received) + 2]
-    held, features, got, made, total, sems = refs[len(received) + 2 :]
+STEPS = (2, 1, 3, 0)
+
+
+def owner(p, q):
+    dp, core = lax.axis_index("dp"), lax.axis_index("row")
+    along_x, along_y = jnp.where(core == 0, p, q), jnp.where(core == 0, q, p)
+    return 4 * (((dp >> 2) + along_y) & 3) + ((dp + along_x) & 3)
+
+
+def product_kernel(p, halves, split, hidden, upstream, *refs):
+    received, refs = refs[: -6 - split * len(halves)], refs[-6 - split * len(halves) :]
+    outs, (held, features, got, made, total, sems) = refs[:-6], refs[-6:]
+    width = HALF * len(halves)
+    owners = [owner(p, q) for q in STEPS]
     loads = [
         pltpu.make_async_copy(
-            hidden.at[:, pl.ds(pl.multiple_of(where[base + i] * LANES, LANES), SPAN)],
+            hidden.at[:, pl.ds(pl.multiple_of(((7 * o) >> 1) * LANES, LANES), SPAN)],
             held.at[i],
             sems.at[i],
         )
-        for i in range(4)
+        for i, o in enumerate(owners)
     ]
-    feature_copy = pltpu.make_async_copy(upstream, features, sems.at[4])
+    feature_copy = pltpu.make_async_copy(
+        upstream.at[:, pl.ds(halves[0] * HALF, width)], features, sems.at[4]
+    )
     got_copies = [
-        pltpu.make_async_copy(received[d], got.at[d], sems.at[5 + d]) for d in range(len(received))
+        pltpu.make_async_copy(a, got.at[d], sems.at[5 + d]) for d, a in enumerate(received)
     ]
     feature_copy.start()
     for copy in loads:
@@ -55,50 +67,58 @@
         copy.start()
     feature_copy.wait()
     stores = []
-    for i in range(4):
+    for i, o in enumerate(owners):
         loads[i].wait()
         total[i % 2] = dot(held[i], features[...])
-        start = pl.multiple_of(where[16 + base + i], 64)
+        start = pl.multiple_of(64 * (o & 1), 64)
         if i == 0:
             for copy in got_copies:
                 copy.wait()
-        for d in range(2):
+        for d in range(len(halves)):
             value = total[i % 2, pl.ds(start, OWN), d * HALF : (d + 1) * HALF]
-            if added:
+            if received:
                 value = value + got[d, i].astype(F32)
             made[d, i] = value.astype(BF16)
-            copy = pltpu.make_async_copy(made.at[d, i], outs[d].at[i], sems.at[7 + 2 * i + d])
+            if split == 2:
+                to = outs[0].at[i] if i < 3 else outs[1]
+            else:
+                to = outs[d].at[i]
+            copy = pltpu.make_async_copy(made.at[d, i], to, sems.at[7 + 2 * i + d])
             copy.start()
             stores.append(copy)
     for copy in stores:
         copy.wait()
 
 
-def product(hidden, upstream, where, base, received=()):
-    tokens, width = upstream.shape
+def product(hidden, upstream, p, halves=(0, 1), received=(), split=1):
+    tokens = hidden.shape[0]
+    count = len(halves)
     piece = jax.ShapeDtypeStruct((4, OWN, HALF), BF16)
+    if split == 2:
+        shapes = (
+            jax.ShapeDtypeStruct((3, OWN, HALF), BF16),
+            jax.ShapeDtypeStruct((OWN, HALF), BF16),
+        )
+    else:
+        shapes = (piece,) * count
     return pl.pallas_call(
-        functools.partial(product_kernel, base, bool(received)),
-        out_shape=(piece, piece),
-        grid_spec=pltpu.PrefetchScalarGridSpec(
-            num_scalar_prefetch=1,
-            grid=(1,),
-            in_specs=[ANY] * (2 + len(received)),
-            out_specs=(ANY, ANY),
-            scratch_shapes=[
-                pltpu.VMEM((4, tokens, SPAN), BF16),
-                pltpu.VMEM((tokens, width), BF16),
-                pltpu.VMEM((2, 4, OWN, HALF) if received else (2, 1, 16, 128), BF16),
-                pltpu.VMEM((2, 4, OWN, HALF), BF16),
-                pltpu.VMEM((2, SPAN, width), F32),
-                pltpu.SemaphoreType.DMA((15,)),
-            ],
-        ),
+        functools.partial(product_kernel, p, halves, split),
+        out_shape=shapes,
+        in_specs=[ANY] * (2 + len(received)),
+        out_specs=(ANY,) * len(shapes),
+        scratch_shapes=[
+            pltpu.VMEM((4, tokens, SPAN), BF16),
+            pltpu.VMEM((tokens, HALF * count), BF16),
+            pltpu.VMEM((count, 4, OWN, HALF) if received else (1, 1, 16, 128), BF16),
+            pltpu.VMEM((count, 4, OWN, HALF), BF16),
+            pltpu.VMEM((2, SPAN, HALF * count), F32),
+            pltpu.SemaphoreType.DMA((15,)),
+        ],
         cost_estimate=pl.CostEstimate(
-            flops=8 * OWN * tokens * width, bytes_accessed=10 << 20, transcendentals=0
+            flops=8 * OWN * tokens * HALF * count, bytes_accessed=10 << 20, transcendentals=0
         ),
         compiler_params=GRANT,
-    )(where, hidden, upstream, *received)
+    )(hidden, upstream, *received)
 
 
 def ring(first_core, k):
@@ -168,25 +188,21 @@
     return (send(far, other(2)), send(up, other(1)), send(down, other(-1)))
 
 
-def add(left, right):
-    return (left.astype(F32) + right.astype(F32)).astype(BF16)
-
-
-def reduced(hidden, upstream, owner):
-    owners = jnp.stack([owner(p, q) for p in (2, 1, 3, 0) for q in (2, 1, 3, 0)])
-    where = jnp.concatenate([(7 * owners) >> 1, 64 * (owners & 1)]).astype(jnp.int32)
-    far_low, far_high = product(hidden, upstream, where, 0)
+def reduced(hidden, upstream):
+    far_low, far_high = product(hidden, upstream, 2)
     from_low = send(far_low, near(1))
     from_high = send(far_high, near(-1))
-    up_low, up_high = product(hidden, upstream, where, 4)
+    (down_low,) = product(hidden, upstream, 3, (0,))
+    direct_low = send(down_low, near(-1))
+    (up_high,) = product(hidden, upstream, 1, (1,))
     direct_high = send(up_high, near(1))
-    down_low, down_high = product(hidden, upstream, where, 8)
-    direct_low = send(down_low, near(-1))
-    added_low = send(add(up_low[:3], from_low[:3]), near(1))
-    added_high = send(add(down_high[:3], from_high[:3]), near(-1))
-    added_low_own = send(add(up_low[3], from_low[3]), near(1))
-    added_high_own = send(add(down_high[3], from_high[3]), near(-1))
-    own_low, own_high = product(hidden, upstream, where, 12, (direct_low, direct_high))
+    most, mine = product(hidden, upstream, 1, (0,), (from_low,), 2)
+    added_low = send(most, near(1))
+    added_low_own = send(mine, near(1))
+    most, mine = product(hidden, upstream, 3, (1,), (from_high,), 2)
+    added_high = send(most, near(-1))
+    added_high_own = send(mine, near(-1))
+    own_low, own_high = product(hidden, upstream, 0, (0, 1), (direct_low, direct_high))
     kept_low, kept_high = in_hbm(own_low), in_hbm(own_high)
     return (
         (own_low[3].astype(F32) + added_low_own.astype(F32), *last(kept_low, added_low)),
@@ -194,7 +210,7 @@
     )
 
 
-TALL = 112
+TALL = 224
 CHUNKS = OWN // TALL
 
 
@@ -350,14 +366,7 @@
 def per_device(
     hidden, upstream, first_codes, first_scale, second_codes, second_rows, second_columns
 ):
-    dp, core = lax.axis_index("dp"), lax.axis_index("row")
-    x, y = dp & 3, dp >> 2
-
-    def owner(p, q):
-        along_x, along_y = jnp.where(core == 0, p, q), jnp.where(core == 0, q, p)
-        return 4 * ((y + along_y) & 3) + ((x + along_x) & 3)
-
-    low, high = reduced(hidden, upstream, owner)
+    low, high = reduced(hidden, upstream)
     rows, columns = second_rows[:, None], second_columns[None, :]
     gradient_low, second_low, row_low, column_low = second_moment(
         0, low, second_codes, rows, columns

time: 129 us -> 127 us (0.984)
  other arithmetic: 11.1 us -> 1.84 us
  Pallas kernels: 50.9 us -> 56.2 us
  waiting for transfers between devices: 20 us -> 23.5 us
  starting transfers between devices: 36.2 us -> 34.1 us
    convert_element_type x4 -> x0, other arithmetic: 8.64 us -> none  [add(): return (left.astype(F32) + right.astype(F32)).astype(BF16)]
    pallas_call x4 -> x6, Pallas kernels: 37.5 us -> 43.5 us  [product(): pl.pallas_call(functools.partial(product_kernel, p, halves, split), out_s...]
    ppermute x14, waiting for transfers between devices: 16.8 us -> 20 us  [send(): return lax.ppermute(value, ('dp', 'row'), pairs)]
    ppermute x14, starting transfers between devices: 22.1 us -> 20.6 us  [send(): return lax.ppermute(value, ('dp', 'row'), pairs)]
  transfers between devices with their start and end apart: 23 -> 23, of which waited for: 8 -> 9; matrix products, arithmetic and copies ran while one was open for 8% -> 2% of each run, Pallas kernels for 31% -> 36%
where the time goes in v3:
time: 127 us
  Pallas kernels  56.2 us (44%)
  starting transfers between devices  34.1 us (27%)
  waiting for transfers between devices  23.5 us (19%)
  local copies, waits for them, and re-layouts  10.1 us (8%)
  other arithmetic  1.84 us (1%)
    pallas_call x6, Pallas kernels, product(): pl.pallas_call(functools.partial(product_kernel, p, halves, split), out_s...  43.5 us
    ppermute x14, starting transfers between devices, send(): return lax.ppermute(value, ('dp', 'row'), pairs)  20.6 us
    ppermute x14, waiting for transfers between devices, send(): return lax.ppermute(value, ('dp', 'row'), pairs)  20 us
    unnamed x41, local copies, waits for them, and re-layouts  10 us
    ppermute x6, starting transfers between devices, ring_max(): parts.append(lax.ppermute(value, axis, way(k)))  7.41 us
    ppermute x2, starting transfers between devices, per_device(): beside = lax.ppermute(row_peak, 'col', [(z, z ^ k) for z in range(4)])  6.07 us
    pallas_call x2, Pallas kernels, last(): pl.pallas_call(sum_kernel, out_shape=(message,) * 3, in_specs=[ANY] * 2,...  4.93 us
    pallas_call x2, Pallas kernels, first_moment(): pl.pallas_call(functools.partial(first_kernel, half), out_shape=(jax.Shap...  4.77 us
  transfers between devices with their start and end apart: 23, of which 9 were waited for; matrix products, arithmetic and copies ran while one was open for 2% of the time, Pallas kernels for 36%

profile of v3, /device:TPU:0, one launch (start us, length us, event | category | flops | bytes accessed | tf_op | source)
XLA Modules:
  0.0 126.7 jit_solution(2927964342126900049)
XLA Ops:
  0.6 8.6 %shard_map.121 = (bf16[4,448,512]{2,1,0:T(8,128)(2,1)}, bf16[4,448,512]{2,1,0:T(8,128)(2,1)}) custom-call(bf16[1024,7168]{1,0:T(8,128)(2,1)} %hidden.11, bf16[1024,1024]{1,0:T(8,128)(2,1)} %upstream.11), custom_call_target="tpu_custom_call" | custom-call | flops 3758096384 | bytes 10485760 | tf_op jit(solution)/shard_map/pallas_call | solution.py:104
  9.2 2.0 %collective-permute-start.8 = (bf16[4,448,512]{2,1,0:T(8,128)(2,1)}, bf16[4,448,512]{2,1,0:T(8,128)(2,1)S(1)}, u32[]{:S(2)}, u32[]{:S(2)}) collective-permute-start(bf16[4,448,512]{2,1,0:T(8,128)(2,1)} %get-tuple-element.42), channel_id=1, source_target_pairs={{0,8},{4,36},{8,16},{12,44},{16,24},{20,52},{24,0},{28,60},{32,40}... | collective-permute-start | bytes 5505032 | tf_op jit(solution)/shard_map/ppermute | solution.py:144
  11.3 1.4 %collective-permute-start.2 = (bf16[4,448,512]{2,1,0:T(8,128)(2,1)}, bf16[4,448,512]{2,1,0:T(8,128)(2,1)}, u32[]{:S(2)}, u32[]{:S(2)}) collective-permute-start(bf16[4,448,512]{2,1,0:T(8,128)(2,1)} %get-tuple-element.35), channel_id=1, source_target_pairs={{0,24},{4,100},{8,0},{12,108},{16,8},{20,116},{24,16},{28,124},{32... | collective-permute-start | bytes 5505032 | tf_op jit(solution)/shard_map/ppermute | solution.py:144
  12.6 5.9 %shard_map.118 = bf16[4,448,512]{2,1,0:T(8,128)(2,1)} custom-call(bf16[1024,7168]{1,0:T(8,128)(2,1)} %hidden.11, bf16[1024,1024]{1,0:T(8,128)(2,1)} %upstream.11), custom_call_target="tpu_custom_call" | custom-call | flops 1879048192 | bytes 10485760 | tf_op jit(solution)/shard_map/pallas_call | solution.py:104
  18.5 1.7 %collective-permute-start = (bf16[4,448,512]{2,1,0:T(8,128)(2,1)}, bf16[4,448,512]{2,1,0:T(8,128)(2,1)S(1)}, u32[]{:S(2)}, u32[]{:S(2)}) collective-permute-start(bf16[4,448,512]{2,1,0:T(8,128)(2,1)} %shard_map.118), channel_id=1, source_target_pairs={{0,24},{4,100},{8,0},{12,108},{16,8},{20,116},{24,16},{28,124},{32... | collective-permute-start | bytes 5505032 | tf_op jit(solution)/shard_map/ppermute | solution.py:144
  20.2 5.9 %shard_map.119 = bf16[4,448,512]{2,1,0:T(8,128)(2,1)} custom-call(bf16[1024,7168]{1,0:T(8,128)(2,1)} %hidden.11, bf16[1024,1024]{1,0:T(8,128)(2,1)} %upstream.11), custom_call_target="tpu_custom_call" | custom-call | flops 1879048192 | bytes 10485760 | tf_op jit(solution)/shard_map/pallas_call | solution.py:104
  26.1 0.3 collective-permute-start.1
  26.4 7.5 %collective-permute-done.8.refs_0_ = bf16[4,448,512]{2,1,0:T(8,128)(2,1)S(1)} collective-permute-done((bf16[4,448,512]{2,1,0:T(8,128)(2,1)}, bf16[4,448,512]{2,1,0:T(8,128)(2,1)S(1)}, u32[]{:S(2)}, u32[]{:S(2)}) %collective-permute-start.8) | collective-permute-done | bytes 1835040 | tf_op jit(solution)/shard_map/ppermute | solution.py:144
  33.9 1.2 copy-done.16
  35.2 6.7 %shard_map.124 = (bf16[3,448,512]{2,1,0:T(8,128)(2,1)}, bf16[448,512]{1,0:T(8,128)(2,1)}) custom-call(bf16[1024,7168]{1,0:T(8,128)(2,1)} %hidden.11, bf16[1024,1024]{1,0:T(8,128)(2,1)} %upstream.11, bf16[4,448,512]{2,1,0:T(8,128)(2,1)} %copy-done.16), custom_call_target="tpu_custom_call" | custom-call | flops 1879048192 | bytes 10485760 | tf_op jit(solution)/shard_map/pallas_call | solution.py:104
  41.9 0.7 collective-permute-start.10
  42.6 6.7 %shard_map.122 = (bf16[3,448,512]{2,1,0:T(8,128)(2,1)}, bf16[448,512]{1,0:T(8,128)(2,1)}) custom-call(bf16[1024,7168]{1,0:T(8,128)(2,1)} %hidden.11, bf16[1024,1024]{1,0:T(8,128)(2,1)} %upstream.11, bf16[4,448,512]{2,1,0:T(8,128)(2,1)} %collective-permute-done.2.refs_0_), custom_call_target="tpu_custom_call" | custom-call | flops 1879048192 | bytes 10485760 | tf_op jit(solution)/shard_map/pallas_call | solution.py:104
  49.4 2.6 %collective-permute-start.4 = (bf16[3,448,512]{2,1,0:T(8,128)(2,1)}, bf16[3,448,512]{2,1,0:T(8,128)(2,1)S(1)}, u32[]{:S(2)}, u32[]{:S(2)}) collective-permute-start(bf16[3,448,512]{2,1,0:T(8,128)(2,1)} %get-tuple-element.37), channel_id=1, source_target_pairs={{0,24},{4,100},{8,0},{12,108},{16,8},{20,116},{24,16},{28,124},{32... | collective-permute-start | bytes 4128776 | tf_op jit(solution)/shard_map/ppermute | solution.py:144
  51.9 0.8 collective-permute-start.3
  52.7 1.6 %collective-permute-done.refs_0_ = bf16[4,448,512]{2,1,0:T(8,128)(2,1)S(1)} collective-permute-done((bf16[4,448,512]{2,1,0:T(8,128)(2,1)}, bf16[4,448,512]{2,1,0:T(8,128)(2,1)S(1)}, u32[]{:S(2)}, u32[]{:S(2)}) %collective-permute-start) | collective-permute-done | bytes 1835040 | tf_op jit(solution)/shard_map/ppermute | solution.py:144
  54.4 1.1 collective-permute-start.9
  55.4 0.1 copy-done.15
  55.6 9.7 %shard_map.120 = (bf16[4,448,512]{2,1,0:T(8,128)(2,1)}, bf16[4,448,512]{2,1,0:T(8,128)(2,1)}) custom-call(bf16[1024,7168]{1,0:T(8,128)(2,1)} %hidden.11, bf16[1024,1024]{1,0:T(8,128)(2,1)} %upstream.11, bf16[4,448,512]{2,1,0:T(8,128)(2,1)} %copy-done.15, bf16[4,448,512]{2,1,0:T(8,128)(2,1)} %collective-permute-done.1.refs_1_), custom_call_target="tpu_custom_call" | custom-call | flops 3758096384 | bytes 10485760 | tf_op jit(solution)/shard_map/pallas_call | solution.py:104
  65.3 3.1 %collective-permute-done.10.got = bf16[3,448,512]{2,1,0:T(8,128)(2,1)S(1)} collective-permute-done((bf16[3,448,512]{2,1,0:T(8,128)(2,1)}, bf16[3,448,512]{2,1,0:T(8,128)(2,1)S(1)}, u32[]{:S(2)}, u32[]{:S(2)}) %collective-permute-start.10) | collective-permute-done | bytes 1376288 | tf_op jit(solution)/shard_map/ppermute | solution.py:144
  68.3 2.3 %shard_map.125 = (bf16[448,512]{1,0:T(8,128)(2,1)S(1)}, bf16[448,512]{1,0:T(8,128)(2,1)}, bf16[448,512]{1,0:T(8,128)(2,1)S(1)}) custom-call(bf16[4,448,512]{2,1,0:T(8,128)(2,1)} %get-tuple-element.41.kept, bf16[3,448,512]{2,1,0:T(8,128)(2,1)S(1)} %collective-permute-done.10.got), custom_call_target="tpu_custom_call" | custom-call | flops 688128 | bytes 4194304 | tf_op jit(solution)/shard_map/pallas_call | solution.py:173
  70.7 0.0 copy-start.19
  70.7 3.4 %collective-permute-start.11 = (bf16[448,512]{1,0:T(8,128)(2,1)S(1)}, bf16[448,512]{1,0:T(8,128)(2,1)S(1)}, u32[]{:S(2)}, u32[]{:S(2)}) collective-permute-start(bf16[448,512]{1,0:T(8,128)(2,1)S(1)} %get-tuple-element.45), channel_id=1, source_target_pairs={{0,64},{4,20},{8,72},{12,28},{16,80},{20,4},{24,88},{28,12},{32,96... | collective-permute-start | bytes 1376264 | tf_op jit(solution)/shard_map/ppermute | solution.py:144
  74.1 0.7 collective-permute-start.12
  74.8 2.6 %collective-permute-start.13 = (bf16[448,512]{1,0:T(8,128)(2,1)S(1)}, bf16[448,512]{1,0:T(8,128)(2,1)S(1)}, u32[]{:S(2)}, u32[]{:S(2)}) collective-permute-start(bf16[448,512]{1,0:T(8,128)(2,1)S(1)} %get-tuple-element.47), channel_id=1, source_target_pairs={{0,96},{4,28},{8,104},{12,4},{16,112},{20,12},{24,120},{28,20},{32... | collective-permute-start | bytes 1376264 | tf_op jit(solution)/shard_map/ppermute | solution.py:144
  77.3 2.6 %shard_map.123 = (bf16[448,512]{1,0:T(8,128)(2,1)}, bf16[448,512]{1,0:T(8,128)(2,1)}, bf16[448,512]{1,0:T(8,128)(2,1)}) custom-call(bf16[4,448,512]{2,1,0:T(8,128)(2,1)} %get-tuple-element.34.kept, bf16[3,448,512]{2,1,0:T(8,128)(2,1)S(1)} %collective-permute-done.4.got), custom_call_target="tpu_custom_call" | custom-call | flops 688128 | bytes 4194304 | tf_op jit(solution)/shard_map/pallas_call | solution.py:173
  79.9 0.0 copy-start.17
  79.9 0.1 collective-permute-start.5
  80.0 0.7 copy-done.17
  80.7 0.2 collective-permute-start.6
  80.9 3.1 %collective-permute-start.7 = (bf16[448,512]{1,0:T(8,128)(2,1)}, bf16[448,512]{1,0:T(8,128)(2,1)S(1)}, u32[]{:S(2)}, u32[]{:S(2)}) collective-permute-start(bf16[448,512]{1,0:T(8,128)(2,1)} %get-tuple-element.40), channel_id=1, source_target_pairs={{0,96},{4,28},{8,104},{12,4},{16,112},{20,12},{24,120},{28,20},{32... | collective-permute-start | bytes 1376264 | tf_op jit(solution)/shard_map/ppermute | solution.py:144
  84.0 0.1 copy.18.rows
  84.2 0.0 copy-start.13
  84.2 1.8 %convert_add_fusion = (f32[448,512]{1,0:T(8,128)S(1)}, f32[448,512]{1,0:T(8,128)S(1)}) fusion(bf16[448,512]{1,0:T(8,128)(2,1)} %collective-permute-done.9, bf16[4,448,512]{2,1,0:T(8,128)(2,1)} %get-tuple-element.41.kept, bf16[448,512]{1,0:T(8,128)(2,1)} %copy-done.17, bf16[4,448,512]{2,1,0:T(8,128)(2,1)} %get-tuple-element.34.kept), kind=kLoop, calls=%fused_computation | loop fusion | flops 1376256 | bytes 3670016 | tf_op jit(solution)/shard_map/add | solution.py:208
  86.0 0.2 collective-permute-done.13.down
  86.2 0.0 copy-done
  86.2 0.8 shard_map.126
  87.0 0.9 copy-done.6
  88.0 2.8 %collective-permute-done.5.far = bf16[448,512]{1,0:T(8,128)(2,1)S(1)} collective-permute-done((bf16[448,512]{1,0:T(8,128)(2,1)}, bf16[448,512]{1,0:T(8,128)(2,1)S(1)}, u32[]{:S(2)}, u32[]{:S(2)}) %collective-permute-start.5) | collective-permute-done | bytes 458784 | tf_op jit(solution)/shard_map/ppermute | solution.py:144
  90.7 4.8 %collective-permute-done.6.up = bf16[448,512]{1,0:T(8,128)(2,1)S(1)} collective-permute-done((bf16[448,512]{1,0:T(8,128)(2,1)}, bf16[448,512]{1,0:T(8,128)(2,1)S(1)}, u32[]{:S(2)}, u32[]{:S(2)}) %collective-permute-start.6) | collective-permute-done | bytes 458784 | tf_op jit(solution)/shard_map/ppermute | solution.py:144
  95.5 0.8 copy-done.8
  96.3 0.8 copy-done.10
  97.1 1.0 copy-done.9
  98.1 1.0 copy-done.11
  99.1 0.8 shard_map.127
  100.0 0.9 copy-done.4
  100.9 1.2 collective-permute-done.16
  102.1 2.0 %collective-permute-start.19 = (f32[1,1024]{1,0:T(1,128)S(1)}, f32[1,1024]{1,0:T(1,128)S(1)}, u32[]{:S(2)}, u32[]{:S(2)}) collective-permute-start(f32[1,1024]{1,0:T(1,128)S(1)} %max.29), channel_id=1, source_target_pairs={{0,24},{4,100},{8,0},{12,108},{16,8},{20,116},{24,16},{28,124},{32... | collective-permute-start | bytes 12296 | tf_op jit(solution)/shard_map/ppermute | solution.py:360
  104.1 0.8 collective-permute-start.18
  104.9 0.5 collective-permute-start.17
  105.4 2.0 %collective-permute-start.14 = (f32[1,448]{1,0:T(1,128)S(1)}, f32[1,448]{1,0:T(1,128)S(1)}, u32[]{:S(2)}, u32[]{:S(2)}) collective-permute-start(f32[1,448]{1,0:T(1,128)S(1)} %get-tuple-element.60), channel_id=1, source_target_pairs={{0,1},{1,0},{2,3},{3,2},{4,5},{5,4},{6,7},{7,6},{8,9},{9,8},{10,11... | collective-permute-start | bytes 5384 | tf_op jit(solution)/shard_map/ppermute | solution.py:381
  107.3 1.9 %collective-permute-done.18 = f32[1,1024]{1,0:T(1,128)S(1)} collective-permute-done((f32[1,1024]{1,0:T(1,128)S(1)}, f32[1,1024]{1,0:T(1,128)S(1)}, u32[]{:S(2)}, u32[]{:S(2)}) %collective-permute-start.18) | collective-permute-done | bytes 4128 | tf_op jit(solution)/shard_map/ppermute | solution.py:360
  109.2 0.5 collective-permute-done.17
  109.7 2.3 %collective-permute-start.22 = (f32[1,1024]{1,0:T(1,128)S(1)}, f32[1,1024]{1,0:T(1,128)S(1)}, u32[]{:S(2)}, u32[]{:S(2)}) collective-permute-start(f32[1,1024]{1,0:T(1,128)S(1)} %maximum_maximum_fusion.1), channel_id=1, source_target_pairs={{0,96},{4,28},{8,104},{12,4},{16,112},{20,12},{24,120},{28,20},{32... | collective-permute-start | bytes 12296 | tf_op jit(solution)/shard_map/ppermute | solution.py:360
  112.1 1.6 %collective-permute-start.21 = (f32[1,1024]{1,0:T(1,128)S(1)}, f32[1,1024]{1,0:T(1,128)S(1)}, u32[]{:S(2)}, u32[]{:S(2)}) collective-permute-start(f32[1,1024]{1,0:T(1,128)S(1)} %maximum_maximum_fusion.1), channel_id=1, source_target_pairs={{0,64},{4,20},{8,72},{12,28},{16,80},{20,4},{24,88},{28,12},{32,96... | collective-permute-start | bytes 12296 | tf_op jit(solution)/shard_map/ppermute | solution.py:360
  113.6 0.2 collective-permute-start.20
  113.8 0.1 copy.20.scale
  114.0 4.1 %collective-permute-start.15 = (f32[1,448]{1,0:T(1,128)S(1)}, f32[1,448]{1,0:T(1,128)S(1)}, u32[]{:S(2)}, u32[]{:S(2)}) collective-permute-start(f32[1,448]{1,0:T(1,128)S(1)} %max.27), channel_id=1, source_target_pairs={{0,3},{1,2},{2,1},{3,0},{4,7},{5,6},{6,5},{7,4},{8,11},{9,10},{10,... | collective-permute-start | bytes 5384 | tf_op jit(solution)/shard_map/ppermute | solution.py:381
  118.1 1.2 copy-done.3
  119.3 1.2 copy-done.7
  120.5 2.4 %shard_map.128 = (f32[448,1024]{1,0:T(8,128)}, bf16[448,1024]{1,0:T(8,128)(2,1)}, f32[8,448]{1,0:T(8,128)S(1)}) custom-call(f32[448,512]{1,0:T(8,128)S(1)} %copy-done.7, f32[448,512]{1,0:T(8,128)S(1)} %copy-done.3, s32[448,1024]{1,0:T(8,128)S(1)} %copy-done.1, f32[448,8]{1,0:T(8,128)S(1)} %copy.20.scale), custom_call_target="tpu_custom_call" | custom-call | flops 9175040 | bytes 5242880 | tf_op jit(solution)/shard_map/pallas_call | solution.py:317
  122.8 2.4 %shard_map.129 = (f32[448,1024]{1,0:T(8,128)}, bf16[448,1024]{1,0:T(8,128)(2,1)}, f32[8,448]{1,0:T(8,128)}) custom-call(f32[448,512]{1,0:T(8,128)S(1)} %copy-done.5, f32[448,512]{1,0:T(8,128)S(1)} %get-tuple-element.51.second.high, s32[448,1024]{1,0:T(8,128)S(1)} %copy-done.1, ...), custom_call_target="tpu_custom_call", output_to_operand_aliasing={{0}: (5, {}), {1}: (6, {})} | custom-call | flops 9175040 | bytes 5242880 | tf_op jit(solution)/shard_map/pallas_call | solution.py:317
  125.3 0.0 copy-start.14
  125.3 0.0 copy-start.12
  125.3 1.3 %norm.1 = bf16[448,1024]{1,0:T(8,128)(2,1)} custom-call(f32[448,512]{1,0:T(8,128)S(1)} %copy-done.3, f32[448,512]{1,0:T(8,128)S(1)} %get-tuple-element.51.second.high, f32[1,448]{1,0:T(1,128)S(1)} %max.28.row_peak, f32[1,1024]{1,0:T(1,128)S(1)} %maximum_maximum_fusion.column_peak), custom_call_target="tpu_custom_call" | custom-call | tf_op jit(solution)/shard_map/norm/pallas_call | solution.py:349
  (43 shorter events, 0.1 us)
Async XLA Ops:
  9.2 24.7 %collective-permute-start.8 = (bf16[4,448,512]{2,1,0:T(8,128)(2,1)}, bf16[4,448,512]{2,1,0:T(8,128)(2,1)S(1)}, u32[]{:S(2)}, u32[]{:S(2)}) collective-permute-start(bf16[4,448,512]{2,1,0:T(8,128)(2,1)} %get-tuple-element.42), channel_id=1, source_target_pairs={{0,8},{4,36},{8,16},{12,44},{16,24},{20,52},{24,0},{28,60},{32,40}... | collective-permute-start | bytes 5505032 | tf_op jit(solution)/shard_map/ppermute | solution.py:144
  11.3 31.4 %collective-permute-start.2 = (bf16[4,448,512]{2,1,0:T(8,128)(2,1)}, bf16[4,448,512]{2,1,0:T(8,128)(2,1)}, u32[]{:S(2)}, u32[]{:S(2)}) collective-permute-start(bf16[4,448,512]{2,1,0:T(8,128)(2,1)} %get-tuple-element.35), channel_id=1, source_target_pairs={{0,24},{4,100},{8,0},{12,108},{16,8},{20,116},{24,16},{28,124},{32... | collective-permute-start | bytes 5505032 | tf_op jit(solution)/shard_map/ppermute | solution.py:144
  18.5 35.9 %collective-permute-start = (bf16[4,448,512]{2,1,0:T(8,128)(2,1)}, bf16[4,448,512]{2,1,0:T(8,128)(2,1)S(1)}, u32[]{:S(2)}, u32[]{:S(2)}) collective-permute-start(bf16[4,448,512]{2,1,0:T(8,128)(2,1)} %shard_map.118), channel_id=1, source_target_pairs={{0,24},{4,100},{8,0},{12,108},{16,8},{20,116},{24,16},{28,124},{32... | collective-permute-start | bytes 5505032 | tf_op jit(solution)/shard_map/ppermute | solution.py:144
  26.1 29.4 %collective-permute-start.1 = (bf16[4,448,512]{2,1,0:T(8,128)(2,1)}, bf16[4,448,512]{2,1,0:T(8,128)(2,1)}, u32[]{:S(2)}, u32[]{:S(2)}) collective-permute-start(bf16[4,448,512]{2,1,0:T(8,128)(2,1)} %shard_map.119), channel_id=1, source_target_pairs={{0,8},{4,36},{8,16},{12,44},{16,24},{20,52},{24,0},{28,60},{32,40}... | collective-permute-start | bytes 5505032 | tf_op jit(solution)/shard_map/ppermute | solution.py:144
  33.9 1.2 copy-start.16
  41.9 26.4 %collective-permute-start.10 = (bf16[3,448,512]{2,1,0:T(8,128)(2,1)}, bf16[3,448,512]{2,1,0:T(8,128)(2,1)S(1)}, u32[]{:S(2)}, u32[]{:S(2)}) collective-permute-start(bf16[3,448,512]{2,1,0:T(8,128)(2,1)} %get-tuple-element.44), channel_id=1, source_target_pairs={{0,8},{4,36},{8,16},{12,44},{16,24},{20,52},{24,0},{28,60},{32,40}... | collective-permute-start | bytes 4128776 | tf_op jit(solution)/shard_map/ppermute | solution.py:144
  49.4 25.4 %collective-permute-start.4 = (bf16[3,448,512]{2,1,0:T(8,128)(2,1)}, bf16[3,448,512]{2,1,0:T(8,128)(2,1)S(1)}, u32[]{:S(2)}, u32[]{:S(2)}) collective-permute-start(bf16[3,448,512]{2,1,0:T(8,128)(2,1)} %get-tuple-element.37), channel_id=1, source_target_pairs={{0,24},{4,100},{8,0},{12,108},{16,8},{20,116},{24,16},{28,124},{32... | collective-permute-start | bytes 4128776 | tf_op jit(solution)/shard_map/ppermute | solution.py:144
  51.9 28.0 %collective-permute-start.3 = (bf16[448,512]{1,0:T(8,128)(2,1)}, bf16[448,512]{1,0:T(8,128)(2,1)S(1)}, u32[]{:S(2)}, u32[]{:S(2)}) collective-permute-start(bf16[448,512]{1,0:T(8,128)(2,1)} %get-tuple-element.36), channel_id=1, source_target_pairs={{0,24},{4,100},{8,0},{12,108},{16,8},{20,116},{24,16},{28,124},{32... | collective-permute-start | bytes 1376264 | tf_op jit(solution)/shard_map/ppermute | solution.py:144
  54.4 1.2 copy-start.15
  54.4 25.7 %collective-permute-start.9 = (bf16[448,512]{1,0:T(8,128)(2,1)}, bf16[448,512]{1,0:T(8,128)(2,1)}, u32[]{:S(2)}, u32[]{:S(2)}) collective-permute-start(bf16[448,512]{1,0:T(8,128)(2,1)} %get-tuple-element.43), channel_id=1, source_target_pairs={{0,8},{4,36},{8,16},{12,44},{16,24},{20,52},{24,0},{28,60},{32,40}... | collective-permute-start | bytes 1376264 | tf_op jit(solution)/shard_map/ppermute | solution.py:144
  70.7 13.3 %copy-start.19 = (f32[448]{0:T(512)S(1)}, f32[448]{0:T(512)}, u32[]{:S(2)}) copy-start(f32[448]{0:T(512)} %param.12) | copy-start | bytes 5380
  70.7 10.2 %collective-permute-start.11 = (bf16[448,512]{1,0:T(8,128)(2,1)S(1)}, bf16[448,512]{1,0:T(8,128)(2,1)S(1)}, u32[]{:S(2)}, u32[]{:S(2)}) collective-permute-start(bf16[448,512]{1,0:T(8,128)(2,1)S(1)} %get-tuple-element.45), channel_id=1, source_target_pairs={{0,64},{4,20},{8,72},{12,28},{16,80},{20,4},{24,88},{28,12},{32,96... | collective-permute-start | bytes 1376264 | tf_op jit(solution)/shard_map/ppermute | solution.py:144
  74.1 11.9 %collective-permute-start.12 = (bf16[448,512]{1,0:T(8,128)(2,1)}, bf16[448,512]{1,0:T(8,128)(2,1)S(1)}, u32[]{:S(2)}, u32[]{:S(2)}) collective-permute-start(bf16[448,512]{1,0:T(8,128)(2,1)} %get-tuple-element.46), channel_id=1, source_target_pairs={{0,32},{4,12},{8,40},{12,20},{16,48},{20,28},{24,56},{28,4},{32,64... | collective-permute-start | bytes 1376264 | tf_op jit(solution)/shard_map/ppermute | solution.py:144
  74.8 11.4 %collective-permute-start.13 = (bf16[448,512]{1,0:T(8,128)(2,1)S(1)}, bf16[448,512]{1,0:T(8,128)(2,1)S(1)}, u32[]{:S(2)}, u32[]{:S(2)}) collective-permute-start(bf16[448,512]{1,0:T(8,128)(2,1)S(1)} %get-tuple-element.47), channel_id=1, source_target_pairs={{0,96},{4,28},{8,104},{12,4},{16,112},{20,12},{24,120},{28,20},{32... | collective-permute-start | bytes 1376264 | tf_op jit(solution)/shard_map/ppermute | solution.py:144
  79.9 0.8 copy-start.17
  79.9 10.8 %collective-permute-start.5 = (bf16[448,512]{1,0:T(8,128)(2,1)}, bf16[448,512]{1,0:T(8,128)(2,1)S(1)}, u32[]{:S(2)}, u32[]{:S(2)}) collective-permute-start(bf16[448,512]{1,0:T(8,128)(2,1)} %get-tuple-element.38), channel_id=1, source_target_pairs={{0,64},{4,20},{8,72},{12,28},{16,80},{20,4},{24,88},{28,12},{32,96... | collective-permute-start | bytes 1376264 | tf_op jit(solution)/shard_map/ppermute | solution.py:144
  80.7 14.8 %collective-permute-start.6 = (bf16[448,512]{1,0:T(8,128)(2,1)}, bf16[448,512]{1,0:T(8,128)(2,1)S(1)}, u32[]{:S(2)}, u32[]{:S(2)}) collective-permute-start(bf16[448,512]{1,0:T(8,128)(2,1)} %get-tuple-element.39), channel_id=1, source_target_pairs={{0,32},{4,12},{8,40},{12,20},{16,48},{20,28},{24,56},{28,4},{32,64... | collective-permute-start | bytes 1376264 | tf_op jit(solution)/shard_map/ppermute | solution.py:144
  80.9 15.4 %collective-permute-start.7 = (bf16[448,512]{1,0:T(8,128)(2,1)}, bf16[448,512]{1,0:T(8,128)(2,1)S(1)}, u32[]{:S(2)}, u32[]{:S(2)}) collective-permute-start(bf16[448,512]{1,0:T(8,128)(2,1)} %get-tuple-element.40), channel_id=1, source_target_pairs={{0,96},{4,28},{8,104},{12,4},{16,112},{20,12},{24,120},{28,20},{32... | collective-permute-start | bytes 1376264 | tf_op jit(solution)/shard_map/ppermute | solution.py:144
  84.1 2.1 %copy-start = (s32[448,1024]{1,0:T(8,128)S(1)}, s32[448,1024]{1,0:T(8,128)}, u32[]{:S(2)}) copy-start(s32[448,1024]{1,0:T(8,128)} %codes.5) | copy-start | bytes 5505028
  84.2 2.0 %copy-start.13 = (f32[1024]{0:T(1024)S(1)}, f32[1024]{0:T(1024)}, u32[]{:S(2)}) copy-start(f32[1024]{0:T(1024)} %param.13) | copy-start | bytes 12292
  87.0 0.9 copy-start.6
  88.0 12.0 %copy-start.2 = (f32[448,512]{1,0:T(8,128)}, f32[448,512]{1,0:T(8,128)S(1)}, u32[]{:S(2)}) copy-start(f32[448,512]{1,0:T(8,128)S(1)} %get-tuple-element.53.second.low) | copy-start | bytes 2752516
  95.5 0.8 copy-start.8
  96.3 0.8 copy-start.10
  97.1 1.0 copy-start.9
  98.1 1.0 copy-start.11
  99.1 14.7 %copy-start.18 = (f32[448,8]{0,1:T(8,128)S(1)}, f32[448,8]{0,1:T(8,128)}, u32[]{:S(2)}) copy-start(f32[448,8]{0,1:T(8,128)} %param.10) | copy-start | bytes 43012
  99.1 19.0 %copy-start.1 = (s32[448,1024]{1,0:T(8,128)S(1)}, s32[448,1024]{1,0:T(8,128)}, u32[]{:S(2)}) copy-start(s32[448,1024]{1,0:T(8,128)} %codes.7) | copy-start | bytes 5505028
  100.0 0.9 copy-start.4
  100.9 1.2 collective-permute-start.16
  102.1 5.3 %collective-permute-start.19 = (f32[1,1024]{1,0:T(1,128)S(1)}, f32[1,1024]{1,0:T(1,128)S(1)}, u32[]{:S(2)}, u32[]{:S(2)}) collective-permute-start(f32[1,1024]{1,0:T(1,128)S(1)} %max.29), channel_id=1, source_target_pairs={{0,24},{4,100},{8,0},{12,108},{16,8},{20,116},{24,16},{28,124},{32... | collective-permute-start | bytes 12296 | tf_op jit(solution)/shard_map/ppermute | solution.py:360
  104.1 5.1 %collective-permute-start.18 = (f32[1,1024]{1,0:T(1,128)S(1)}, f32[1,1024]{1,0:T(1,128)S(1)}, u32[]{:S(2)}, u32[]{:S(2)}) collective-permute-start(f32[1,1024]{1,0:T(1,128)S(1)} %max.29), channel_id=1, source_target_pairs={{0,16},{4,68},{8,24},{12,76},{16,0},{20,84},{24,8},{28,92},{32,48}... | collective-permute-start | bytes 12296 | tf_op jit(solution)/shard_map/ppermute | solution.py:360
  104.9 4.8 %collective-permute-start.17 = (f32[1,1024]{1,0:T(1,128)S(1)}, f32[1,1024]{1,0:T(1,128)S(1)}, u32[]{:S(2)}, u32[]{:S(2)}) collective-permute-start(f32[1,1024]{1,0:T(1,128)S(1)} %max.29), channel_id=1, source_target_pairs={{0,8},{4,36},{8,16},{12,44},{16,24},{20,52},{24,0},{28,60},{32,40}... | collective-permute-start | bytes 12296 | tf_op jit(solution)/shard_map/ppermute | solution.py:360
  105.4 8.6 %collective-permute-start.14 = (f32[1,448]{1,0:T(1,128)S(1)}, f32[1,448]{1,0:T(1,128)S(1)}, u32[]{:S(2)}, u32[]{:S(2)}) collective-permute-start(f32[1,448]{1,0:T(1,128)S(1)} %get-tuple-element.60), channel_id=1, source_target_pairs={{0,1},{1,0},{2,3},{3,2},{4,5},{5,4},{6,7},{7,6},{8,9},{9,8},{10,11... | collective-permute-start | bytes 5384 | tf_op jit(solution)/shard_map/ppermute | solution.py:381
  109.7 15.6 %collective-permute-start.22 = (f32[1,1024]{1,0:T(1,128)S(1)}, f32[1,1024]{1,0:T(1,128)S(1)}, u32[]{:S(2)}, u32[]{:S(2)}) collective-permute-start(f32[1,1024]{1,0:T(1,128)S(1)} %maximum_maximum_fusion.1), channel_id=1, source_target_pairs={{0,96},{4,28},{8,104},{12,4},{16,112},{20,12},{24,120},{28,20},{32... | collective-permute-start | bytes 12296 | tf_op jit(solution)/shard_map/ppermute | solution.py:360
  112.1 13.2 %collective-permute-start.21 = (f32[1,1024]{1,0:T(1,128)S(1)}, f32[1,1024]{1,0:T(1,128)S(1)}, u32[]{:S(2)}, u32[]{:S(2)}) collective-permute-start(f32[1,1024]{1,0:T(1,128)S(1)} %maximum_maximum_fusion.1), channel_id=1, source_target_pairs={{0,64},{4,20},{8,72},{12,28},{16,80},{20,4},{24,88},{28,12},{32,96... | collective-permute-start | bytes 12296 | tf_op jit(solution)/shard_map/ppermute | solution.py:360
  113.6 11.7 %collective-permute-start.20 = (f32[1,1024]{1,0:T(1,128)S(1)}, f32[1,1024]{1,0:T(1,128)S(1)}, u32[]{:S(2)}, u32[]{:S(2)}) collective-permute-start(f32[1,1024]{1,0:T(1,128)S(1)} %maximum_maximum_fusion.1), channel_id=1, source_target_pairs={{0,32},{4,12},{8,40},{12,20},{16,48},{20,28},{24,56},{28,4},{32,64... | collective-permute-start | bytes 12296 | tf_op jit(solution)/shard_map/ppermute | solution.py:360
  114.0 11.3 %collective-permute-start.15 = (f32[1,448]{1,0:T(1,128)S(1)}, f32[1,448]{1,0:T(1,128)S(1)}, u32[]{:S(2)}, u32[]{:S(2)}) collective-permute-start(f32[1,448]{1,0:T(1,128)S(1)} %max.27), channel_id=1, source_target_pairs={{0,3},{1,2},{2,1},{3,0},{4,7},{5,6},{6,5},{7,4},{8,11},{9,10},{10,... | collective-permute-start | bytes 5384 | tf_op jit(solution)/shard_map/ppermute | solution.py:381
  118.1 1.2 copy-start.3
  119.3 1.2 copy-start.7
  120.5 2.4 %copy-start.5 = (f32[448,512]{1,0:T(8,128)S(1)}, f32[448,512]{1,0:T(8,128)}, u32[]{:S(2)}) copy-start(f32[448,512]{1,0:T(8,128)} %copy-done.4) | copy-start | bytes 2752516
  125.3 1.4 %copy-start.14 = (f32[1,448]{1,0:T(1,128)}, f32[1,448]{1,0:T(1,128)S(1)}, u32[]{:S(2)}) copy-start(f32[1,448]{1,0:T(1,128)S(1)} %max.28.row_peak) | copy-start | bytes 5380
  125.3 1.3 %copy-start.12 = (f32[1,1024]{1,0:T(1,128)}, f32[1,1024]{1,0:T(1,128)S(1)}, u32[]{:S(2)}) copy-start(f32[1,1024]{1,0:T(1,128)S(1)} %maximum_maximum_fusion.column_peak) | copy-start | bytes 12292
